TPU v7x, 256 devices: a whole 4x4x8 slice. The times are simulated.
256 devices in a mesh: tile: 64 (over x, y, z_lo), slab: 4 (over z_hi, core).
Axes of the slice: x: 4, y: 4, z: 8 (z_hi: 2, z_lo: 4; z = z_hi * 4 + z_lo), core: 2. Of those that a mesh axis runs over, the one named last changes fastest.
Arguments:
- kernels: float32 [64, 3, 64, 128, 128], P('tile', None, 'slab'), may hold values from -60 to 60
- volume: float32 [64, 64, 128, 128], P('tile', 'slab'), may hold values from 0.25 to 4
- neighbours: int32 [64, 4], replicated, may hold values from 0 to 63, as said below
- glued_sides: int32 [64, 4], replicated, may hold values from 0 to 3
- reversals: int32 [64, 4], replicated, may hold values from 0 to 1, as said below
Outputs:
- smoothed: float32 [64, 3, 64, 128, 128], P('tile', None, 'slab')
Inputs may be any that keep to these rules, and one draw needn't show every extreme that they name: Each side of each tile is glued to exactly one side of some tile (possibly another side of the same tile), and the gluing is symmetric: side glued_sides[t, s] of tile neighbours[t, s] is glued back to side s of tile t. The gluing is known only at run time. `reversals`: the two sides of a glued pair carry the same code.
All inputs are finite; a program needn't handle non-finite values.
Results may differ from a plain program's by a relative error of at most 0.000073.
Values sent between devices are 32-bit elements; how exact they have to be, the bound alone decides.
No kernel may reach another device: no remote copies, remote signals or barrier semaphores. Data moves between devices by JAX's collectives and lax.ppermute only.
A program may use at most 128 MiB of HBM per device.

v0:
```python
import functools
import math

import jax
import jax.numpy as jnp
import numpy as np
from jax import lax
from jax.experimental import pallas as pl
from jax.experimental.pallas import tpu as pltpu
from jax.sharding import PartitionSpec as P

SIDE = 128
HALF = 15
DEEP = 16
OWN = 16
SPAN = 2 * HALF + OWN
F32 = jnp.float32
BF16 = jnp.bfloat16

TAPS = [float(np.float32(math.exp(-k * k / 50.0))) for k in range(HALF + 1)]


def tap(offset):
    offset = np.abs(np.asarray(offset))
    return np.where(offset <= HALF, np.exp(-(offset.astype(np.float64) ** 2) / 50.0), 0.0).astype(np.float32)


def halves(values):
    high = values.astype(BF16)
    low = (values - high.astype(np.float32)).astype(BF16)
    return high, low


def constants():
    cell = np.arange(SIDE)
    deep = np.arange(DEEP)
    live = (deep < HALF)[:, None]
    square = tap(cell[:, None] - cell[None, :])
    high, low = halves(square)
    pair = np.block([[high, low], [high, np.zeros_like(low)]])
    near = tap(cell[None, :] + deep[:, None] + 1) * live
    far = tap(SIDE - cell[None, :] + deep[:, None]) * live
    pick_west = (cell[None, :] == deep[:, None]).astype(np.float32) * live
    pick_east = (cell[None, :] == SIDE - 1 - deep[:, None]).astype(np.float32) * live
    sum_west = tap(cell[None, :] - deep[:, None]) * live
    sum_east = tap(cell[None, :] - (SIDE - 1 - deep[:, None])) * live
    picks = np.stack([pick_west, pick_east, sum_west, sum_east])
    back = tap(deep[:, None] + deep[None, :] + 1) * live * live.T
    south_own = near.T.astype(np.float64) @ back
    north_own = (far.T.astype(np.float64) @ back)[:, ::-1]
    along = np.concatenate([square, near.T, far.T, south_own, north_own], axis=1).astype(np.float32)
    eye = np.eye(8, dtype=np.float32)
    spread = np.concatenate([np.kron(eye, near), np.kron(eye, far)], axis=0)
    corner = np.kron(np.eye(4, dtype=np.float32), np.concatenate([near, far], axis=0))
    ends = np.concatenate([pick_west, pick_east], axis=0)
    return dict(
        pair=pair,
        picks=picks,
        along=along,
        spread=np.stack(halves(spread)),
        corner=np.stack(halves(corner)),
        ends=ends.astype(BF16),
    )


def split(values):
    high = values.astype(BF16)
    return high, (values - high.astype(F32)).astype(BF16)


def dot(left, right):
    return jnp.dot(left, right, preferred_element_type=F32)


def dot_t(left, right):
    return lax.dot_general(left, right, (((1,), (1,)), ((), ())), preferred_element_type=F32)


def through(rows, pair):
    high, low = split(rows)
    both = dot(jnp.concatenate([high, low], axis=1), pair)
    return both[:, :SIDE] + both[:, SIDE:]


def radial_kernel(weighted, *refs):
    out = refs[-1]
    parts = refs[:-1]
    rows = out.shape[1]

    def tile(i, carry):
        at = pl.ds(pl.multiple_of(i * 8, 8), 8)

        def level(j):
            part, k = (0, j) if j < HALF else (1, j - HALF) if j < HALF + OWN else (2, j - HALF - OWN)
            x = parts[part][k, at, :]
            return x * parts[part + 3][k, at, :] if weighted else x

        x = [level(j) for j in range(SPAN)]
        for m in range(OWN):
            c = m + HALF
            total = TAPS[0] * x[c]
            for k in range(1, HALF + 1):
                total = total + TAPS[k] * (x[c - k] + x[c + k])
            out[m, at, :] = total
        return carry

    lax.fori_loop(0, rows // 8, tile, 0)


def radial(parts, weights):
    weighted = weights is not None
    arrays = list(parts) + (list(weights) if weighted else [])
    block = 32
    return pl.pallas_call(
        functools.partial(radial_kernel, weighted),
        grid=(SIDE // block,),
        in_specs=[pl.BlockSpec((a.shape[0], block, SIDE), lambda i: (0, i, 0)) for a in arrays],
        out_specs=pl.BlockSpec((OWN, block, SIDE), lambda i: (0, i, 0)),
        out_shape=jax.ShapeDtypeStruct((OWN, SIDE, SIDE), F32),
        name="radial",
        cost_estimate=pl.CostEstimate(flops=OWN * SPAN * SIDE * SIDE * 2, bytes_accessed=7 << 20, transcendentals=0),
    )(*arrays)


def pack_kernel(field_count, glued, pair, picks, *refs):
    fields = refs[:field_count]
    out, edge = refs[field_count:]

    def choose(side):
        raw = jnp.where(glued[side] < 2, 1.0, 0.0).astype(F32)
        return picks[side] * raw + picks[side + 2] * (1.0 - raw)

    left_high, left_low = split(jnp.concatenate([choose(0), choose(1)], axis=0))
    left = jnp.concatenate([left_high, left_low], axis=0)
    for f in range(field_count):
        rows = fields[f]
        mine = pl.ds(f * OWN, OWN)
        for d in range(DEEP):
            edge[pl.ds(d, OWN, stride=DEEP), :] = rows[pl.ds(d, OWN, stride=SIDE), :]
            edge[pl.ds(OWN * DEEP + d, OWN, stride=DEEP), :] = rows[pl.ds(SIDE - 1 - d, OWN, stride=SIDE), :]
        raw = edge[...]
        across = through(raw, pair[...])
        for side in (2, 3):
            at = slice((side - 2) * OWN * DEEP, (side - 1) * OWN * DEEP)
            strip = jnp.where(glued[side] < 2, raw[at], across[at])
            out[mine, side, :, :] = strip.reshape(OWN, DEEP, SIDE)
        high, low = split(rows[...])
        both = dot_t(left, high)
        strips = both[: 2 * DEEP] + both[2 * DEEP :] + dot_t(left_high, low)
        for q in range(OWN):
            plane = strips[:, q * SIDE : (q + 1) * SIDE]
            out[f * OWN + q, 0, :, :] = plane[:DEEP]
            out[f * OWN + q, 1, :, :] = plane[DEEP:]


VMEM = pl.BlockSpec(memory_space=pltpu.VMEM)
SMEM = pl.BlockSpec(memory_space=pltpu.SMEM)


def pack(fields, glued, const):
    count = len(fields)
    return pl.pallas_call(
        functools.partial(pack_kernel, count),
        in_specs=[SMEM] + [VMEM] * (2 + count),
        out_specs=VMEM,
        out_shape=jax.ShapeDtypeStruct((count * OWN, 4, DEEP, SIDE), F32),
        scratch_shapes=[pltpu.VMEM((2 * OWN * DEEP, SIDE), F32)],
        name="pack",
        cost_estimate=pl.CostEstimate(flops=1 << 29, bytes_accessed=6 << 20, transcendentals=0),
    )(glued, const["pair"], const["picks"], *[f.reshape(OWN * SIDE, SIDE) for f in fields])


def route_kernel(source, fix, ends, corner, flipped, strips, out, patch):
    tiles = out.shape[0]
    group = 4

    def move(i, carry):
        for j in range(8):
            e = i * 8 + j
            t, s = i * 2 + j // 4, j % 4
            out[t, s, :, :] = strips[source[e], :, :]
        return carry

    lax.fori_loop(0, tiles // 2, move, 0)
    margins = out[:, 0:2, :, :].reshape(tiles * 2 * DEEP, SIDE)
    high, low = split(margins)
    seen = dot_t(ends[...], high) + dot_t(ends[...], low)
    first, last = seen[:DEEP], seen[DEEP:]
    swap = flipped[...] > 0.5
    turned = jnp.concatenate([jnp.where(swap, last, first), jnp.where(swap, first, last)], axis=0)
    high, low = split(turned)
    for g in range(tiles // group):
        at = slice(g * SIDE, (g + 1) * SIDE)
        added = dot(high[:, at], corner[0]) + dot(high[:, at], corner[1]) + dot(low[:, at], corner[0])
        for j in range(group):
            block = added[:, j * SIDE : (j + 1) * SIDE]
            patch[(g * group + j) * 2] = block[:DEEP]
            patch[(g * group + j) * 2 + 1] = block[DEEP:]
    patch[tiles * 2] = jnp.zeros((DEEP, SIDE), F32)

    def mend(i, carry):
        for j in range(4):
            t, s = i * 2 + j // 2, 2 + j % 2
            out[t, s, :, :] = out[t, s, :, :] + patch[fix[i * 4 + j], :, :]
        return carry

    lax.fori_loop(0, tiles // 2, mend, 0)


def route(strips, tables, const):
    tiles = strips.shape[0]
    source, fix, flipped = tables
    return pl.pallas_call(
        route_kernel,
        in_specs=[SMEM, SMEM] + [VMEM] * 4,
        out_specs=VMEM,
        out_shape=jax.ShapeDtypeStruct((tiles, 4, DEEP, SIDE), F32),
        scratch_shapes=[pltpu.VMEM((tiles * 2 + 1, DEEP, SIDE), F32)],
        name="route",
        cost_estimate=pl.CostEstimate(flops=1 << 28, bytes_accessed=4 << 20, transcendentals=0),
    )(source, fix, const["ends"], const["corner"], flipped, strips.reshape(tiles * 4, DEEP, SIDE))


def turn(code):
    row = lax.broadcasted_iota(jnp.int32, (SIDE, SIDE), 0)
    col = lax.broadcasted_iota(jnp.int32, (SIDE, SIDE), 1)
    return jnp.where(col == jnp.where(code == 1, SIDE - 1 - row, row), 1.0, 0.0).astype(BF16)


def finish_kernel(glued, turned, pair, along, spread, margins, *refs):
    fields = refs[:4]
    out, rows, across, below = refs[4:]
    f = pl.program_id(0)
    for k in range(4):

        @pl.when(f == k)
        def _():
            rows[...] = fields[k][...]

    size = OWN * DEEP
    across[...] = through(rows[...], pair[...]).reshape(OWN, SIDE, SIDE)
    sides = []
    for side in (0, 1):
        high, low = split(margins[:, side, :, :].reshape(size, SIDE))
        way = turn(turned[side])
        sides.append(dot_t(way, high) + dot_t(way, low))
    for g in range(2):
        at = slice(g * SIDE, (g + 1) * SIDE)
        high, low = split(jnp.concatenate([sides[0][:, at], sides[1][:, at]], axis=1))
        for q in range(0, 8, 2):
            to = slice(q * SIDE, (q + 2) * SIDE)
            added = dot(high, spread[0, :, to]) + dot(high, spread[1, :, to]) + dot(low, spread[0, :, to])
            across[g * 8 + q] += added[:, :SIDE]
            across[g * 8 + q + 1] += added[:, SIDE:]
    ahead = []
    for side in (2, 3):
        high, low = split(margins[:, side, :, :].reshape(size, SIDE))
        way = turn(turned[side])
        ahead.append((dot(high, way) + dot(low, way)).reshape(OWN, DEEP, SIDE))
    lane = lax.broadcasted_iota(jnp.int32, (SIDE, along.shape[1]), 1)
    south = jnp.where(glued[2] < 2, 1.0, 0.0).astype(F32)
    north = jnp.where(glued[3] < 2, 1.0, 0.0).astype(F32)
    first_own = SIDE + 2 * DEEP
    scale = jnp.where(lane < first_own, 1.0, jnp.where(lane < first_own + DEEP, south, north))
    left_high, left_low = split(along[...] * scale)
    left = jnp.concatenate([left_high, left_low], axis=0)

    def column(q):
        base = q * SIDE
        return jnp.concatenate(
            [across[q], ahead[0][q], ahead[1][q], rows[base : base + DEEP, :], rows[base + SIDE - DEEP : base + SIDE, :]],
            axis=0,
        )

    for q in range(0, OWN, 2):
        high, low = split(jnp.concatenate([column(q), column(q + 1)], axis=1))
        both = dot(left, high)
        total = both[:SIDE] + both[SIDE:] + dot(left_high, low)
        for j in range(2):
            plane = total[:, j * SIDE : (j + 1) * SIDE]

            @pl.when(f == 0)
            def _():
                below[q + j] = plane

            @pl.when(f > 0)
            def _():
                out[0, q + j] = plane / below[q + j]


def finish(fields, margins, glued, turned, const):
    whole = [pl.BlockSpec((OWN * SIDE, SIDE), lambda i: (0, 0)) for _ in range(4)]
    return pl.pallas_call(
        finish_kernel,
        grid=(4,),
        in_specs=[SMEM, SMEM]
        + [
            pl.BlockSpec(const["pair"].shape, lambda i: (0, 0)),
            pl.BlockSpec(const["along"].shape, lambda i: (0, 0)),
            pl.BlockSpec(const["spread"].shape, lambda i: (0, 0, 0)),
            pl.BlockSpec((OWN, 4, DEEP, SIDE), lambda i: (i, 0, 0, 0)),
        ]
        + whole,
        out_specs=pl.BlockSpec((1, OWN, SIDE, SIDE), lambda i: (jnp.maximum(i - 1, 0), 0, 0, 0)),
        out_shape=jax.ShapeDtypeStruct((3, OWN, SIDE, SIDE), F32),
        scratch_shapes=[
            pltpu.VMEM((OWN * SIDE, SIDE), F32),
            pltpu.VMEM((OWN, SIDE, SIDE), F32),
            pltpu.VMEM((OWN, SIDE, SIDE), F32),
        ],
        name="finish",
        cost_estimate=pl.CostEstimate(flops=1 << 32, bytes_accessed=10 << 20, transcendentals=0),
    )(
        glued,
        turned,
        const["pair"],
        const["along"],
        const["spread"],
        margins,
        *[f.reshape(OWN * SIDE, SIDE) for f in fields],
    )


UP = [(0, 1), (1, 2), (2, 3)]
DOWN = [(1, 0), (2, 1), (3, 2)]


def with_halo(levels):
    below = lax.ppermute(levels[1:], "slab", UP)
    above = lax.ppermute(levels[:-1], "slab", DOWN)
    return below, levels, above


def per_device(kernels, volume, neighbours, glued_sides, reversals):
    const = {k: jnp.asarray(v) for k, v in constants().items()}
    tile = lax.axis_index("tile")
    glued = glued_sides[tile]
    turned = reversals[tile]
    tiles = neighbours.shape[0]
    source = (neighbours * 4 + glued_sides).reshape(-1)
    ahead = glued_sides[:, 2:]
    fix = jnp.where(ahead >= 2, neighbours[:, 2:] * 2 + ahead - 2, tiles * 2).reshape(-1)
    flipped = jnp.repeat(reversals[:, :2].astype(F32).reshape(-1), DEEP)[None, :]
    tables = (source, fix, flipped)

    weights = with_halo(volume[0])
    fields = [radial(weights, None)]
    for f in range(3):
        fields.append(radial(with_halo(kernels[0, f]), weights))
    strips = pack(fields, glued, const)
    routed_in = lax.all_to_all(strips, "tile", split_axis=0, concat_axis=0, tiled=True)
    picked = route(routed_in, tables, const)
    margins = lax.all_to_all(picked, "tile", split_axis=0, concat_axis=0, tiled=True)
    return finish(fields, margins, glued, turned, const)[None]


def solution(mesh):
    placed = (P("tile", None, "slab", None, None), P("tile", "slab", None, None), P(), P(), P())
    return jax.shard_map(
        per_device,
        mesh=mesh,
        in_specs=placed,
        out_specs=P("tile", None, "slab", None, None),
        check_vma=False,
    )
```

profile of v0, /device:TPU:1, one launch (start us, length us, event | category | flops | bytes accessed | tf_op | source)
XLA Modules:
  0.0 254.0 jit_solution(2728222784110318019)
XLA Ops:
  0.0 5.1 %slice_bitcast_fusion.3 = (f32[15,128,128]{2,1,0:T(8,128)}, f32[15,128,128]{2,1,0:T(8,128)S(1)}, f32[15,128,128]{2,1,0:T(8,128)}, f32[15,128,128]{2,1,0:T(8,128)...) fusion(f32[1,3,16,128,128]{4,3,2,1,0:T(8,128)} %param.11), kind=kLoop, calls=%fused_computation.3 | loop fusion | bytes 11796480 | tf_op jit(solution)/shard_map/slice | solution.py:330
  5.1 10.4 %collective-permute-start.6 = (f32[15,128,128]{2,1,0:T(8,128)S(1)}, f32[15,128,128]{2,1,0:T(8,128)}, u32[]{:S(2)}, u32[]{:S(2)}) collective-permute-start(f32[15,128,128]{2,1,0:T(8,128)S(1)} %get-tuple-element.6), channel_id=1, source_target_pairs={{0,1},{1,2},{2,3},{4,5},{5,6},{6,7},{8,9},{9,10},{10,11},{12,13},{... | collective-permute-start | bytes 2949128 | tf_op jit(solution)/shard_map/ppermute | solution.py:329
  15.8 1.9 collective-permute-start
  17.7 3.4 %collective-permute-start.1 = (f32[15,128,128]{2,1,0:T(8,128)S(1)}, f32[15,128,128]{2,1,0:T(8,128)}, u32[]{:S(2)}, u32[]{:S(2)}) collective-permute-start(f32[15,128,128]{2,1,0:T(8,128)S(1)} %get-tuple-element.14), channel_id=1, source_target_pairs={{1,0},{2,1},{3,2},{5,4},{6,5},{7,6},{9,8},{10,9},{11,10},{13,12},{... | collective-permute-start | bytes 2949128 | tf_op jit(solution)/shard_map/ppermute | solution.py:330
  21.1 1.9 collective-permute-start.7
  23.0 7.6 %collective-permute-start.4 = (f32[15,128,128]{2,1,0:T(8,128)}, f32[15,128,128]{2,1,0:T(8,128)}, u32[]{:S(2)}, u32[]{:S(2)}) collective-permute-start(f32[15,128,128]{2,1,0:T(8,128)} %get-tuple-element.8), channel_id=1, source_target_pairs={{0,1},{1,2},{2,3},{4,5},{5,6},{6,7},{8,9},{9,10},{10,11},{12,13},{... | collective-permute-start | bytes 2949128 | tf_op jit(solution)/shard_map/ppermute | solution.py:329
  30.6 1.9 collective-permute-start.5
  32.5 7.9 %collective-permute-done.refs_0_.refs_3_ = f32[15,128,128]{2,1,0:T(8,128)} collective-permute-done((f32[15,128,128]{2,1,0:T(8,128)S(1)}, f32[15,128,128]{2,1,0:T(8,128)}, u32[]{:S(2)}, u32[]{:S(2)}) %collective-permute-start) | collective-permute-done | bytes 983072 | tf_op jit(solution)/shard_map/ppermute | solution.py:329
  40.5 8.5 %collective-permute-start.2 = (f32[15,128,128]{2,1,0:T(8,128)}, f32[15,128,128]{2,1,0:T(8,128)}, u32[]{:S(2)}, u32[]{:S(2)}) collective-permute-start(f32[15,128,128]{2,1,0:T(8,128)} %get-tuple-element.10), channel_id=1, source_target_pairs={{0,1},{1,2},{2,3},{4,5},{5,6},{6,7},{8,9},{9,10},{10,11},{12,13},{... | collective-permute-start | bytes 2949128 | tf_op jit(solution)/shard_map/ppermute | solution.py:329
  49.0 1.9 collective-permute-start.3
  51.7 1.7 slice_bitcast_fusion
  53.4 4.6 %radial.4 = f32[16,128,128]{2,1,0:T(8,128)} custom-call(f32[15,128,128]{2,1,0:T(8,128)} %collective-permute-done.refs_0_.refs_3_, f32[16,128,128]{2,1,0:T(8,128)} %bitcast.29, f32[15,128,128]{2,1,0:T(8,128)} %collective-permute-done.1.refs_2_.refs_5_), custom_call_target="tpu_custom_call" | custom-call | flops 24117248 | bytes 7340032 | tf_op jit(solution)/shard_map/radial/pallas_call | solution.py:114
  58.0 5.4 %radial.7 = f32[16,128,128]{2,1,0:T(8,128)} custom-call(f32[15,128,128]{2,1,0:T(8,128)} %collective-permute-done.6.refs_0_, f32[16,128,128]{2,1,0:T(8,128)} %get-tuple-element.11.refs_1_, f32[15,128,128]{2,1,0:T(8,128)} %collective-permute-done.7.refs_2_, f32[15,128,128]{2,1,0:T(8,128)} %collective-permute-done.refs_0_.refs_3_, f32[16,128,128]{2,1,0:T(8,128)} %bitcast.30, ...), custom_call_target="tpu_custom_call" | custom-call | flops 24117248 | bytes 7340032 | tf_op jit(solution)/shard_map/radial/pallas_call | solution.py:114
  63.4 6.0 %collective-permute-done.5.refs_2_ = f32[15,128,128]{2,1,0:T(8,128)} collective-permute-done((f32[15,128,128]{2,1,0:T(8,128)}, f32[15,128,128]{2,1,0:T(8,128)}, u32[]{:S(2)}, u32[]{:S(2)}) %collective-permute-start.5) | collective-permute-done | bytes 983072 | tf_op jit(solution)/shard_map/ppermute | solution.py:330
  69.4 5.4 %radial.6 = f32[16,128,128]{2,1,0:T(8,128)} custom-call(f32[15,128,128]{2,1,0:T(8,128)} %collective-permute-done.4.refs_0_, f32[16,128,128]{2,1,0:T(8,128)} %get-tuple-element.12.refs_1_, f32[15,128,128]{2,1,0:T(8,128)} %collective-permute-done.5.refs_2_, f32[15,128,128]{2,1,0:T(8,128)} %collective-permute-done.refs_0_.refs_3_, f32[16,128,128]{2,1,0:T(8,128)} %bitcast.31, ...), custom_call_target="tpu_custom_call" | custom-call | flops 24117248 | bytes 7340032 | tf_op jit(solution)/shard_map/radial/pallas_call | solution.py:114
  74.8 35.6 %collective-permute-done.3.refs_2_ = f32[15,128,128]{2,1,0:T(8,128)} collective-permute-done((f32[15,128,128]{2,1,0:T(8,128)}, f32[15,128,128]{2,1,0:T(8,128)}, u32[]{:S(2)}, u32[]{:S(2)}) %collective-permute-start.3) | collective-permute-done | bytes 983072 | tf_op jit(solution)/shard_map/ppermute | solution.py:330
  110.5 5.4 %radial.5 = f32[16,128,128]{2,1,0:T(8,128)} custom-call(f32[15,128,128]{2,1,0:T(8,128)} %collective-permute-done.2.refs_0_, f32[16,128,128]{2,1,0:T(8,128)} %get-tuple-element.13.refs_1_, f32[15,128,128]{2,1,0:T(8,128)} %collective-permute-done.3.refs_2_, f32[15,128,128]{2,1,0:T(8,128)} %collective-permute-done.refs_0_.refs_3_, f32[16,128,128]{2,1,0:T(8,128)} %bitcast.32, ...), custom_call_target="tpu_custom_call" | custom-call | flops 24117248 | bytes 7340032 | tf_op jit(solution)/shard_map/radial/pallas_call | solution.py:114
  115.9 5.5 %pack.1 = f32[64,4,16,128]{3,2,1,0:T(8,128)} custom-call(s32[4]{0:T(128)} %dynamic-slice_reduce_fusion.1.glued, bf16[256,256]{1,0:T(8,128)(2,1)} %constant.30.clone.pair, f32[4,16,128]{2,1,0:T(8,128)} %constant.31.clone.picks, f32[2048,128]{1,0:T(8,128)} %bitcast.40, f32[2048,128]{1,0:T(8,128)} %bitcast.38, f32[2048,128]{1,0:T(8,128)} %bitcast.36, ...), custom_call_target="tpu_custom_call" | custom-call | flops 536870912 | bytes 6291456 | tf_op jit(solution)/shard_map/pack/pallas_call | solution.py:162
  121.4 10.4 %all-to-all-start = ((f32[64,4,16,128]{3,2,1,0:T(8,128)}), f32[64,4,16,128]{3,2,1,0:T(8,128)S(1)}, u32[]{:S(2)}, u32[]{:S(2)}) async-start(f32[64,4,16,128]{3,2,1,0:T(8,128)} %pack.1), calls=%async_computation | async-start | bytes 4194304 | tf_op jit(solution)/shard_map/all_to_all | solution.py:351
  134.4 40.2 %all-to-all-done = f32[64,4,16,128]{3,2,1,0:T(8,128)S(1)} async-done(((f32[64,4,16,128]{3,2,1,0:T(8,128)}), f32[64,4,16,128]{3,2,1,0:T(8,128)S(1)}, u32[]{:S(2)}, u32[]{:S(2)}) %all-to-all-start) | async-done | bytes 2097184 | tf_op jit(solution)/shard_map/all_to_all | solution.py:351
  175.9 5.2 %route.1 = f32[64,4,16,128]{3,2,1,0:T(8,128)} custom-call(s32[256]{0:T(256)} %reshape.36.source, s32[128]{0:T(128)} %reshape.37.fix, bf16[32,128]{1,0:T(8,128)(2,1)} %constant.35.clone.ends, bf16[2,128,512]{2,1,0:T(8,128)(2,1)} %constant.34.clone.corner, f32[1,2048]{1,0:T(1,128)} %broadcast_in_dim_reshape.3.flipped, f32[256,16,128]{2,1,0:T(8,128)} %bitcast.33), custom_call_target="tpu_custom_call" | custom-call | flops 268435456 | bytes 4194304 | tf_op jit(solution)/shard_map/route/pallas_call | solution.py:213
  181.0 4.7 %all-to-all-start.1 = ((f32[64,4,16,128]{3,2,1,0:T(8,128)}), f32[64,4,16,128]{3,2,1,0:T(8,128)S(1)}, u32[]{:S(2)}, u32[]{:S(2)}) async-start(f32[64,4,16,128]{3,2,1,0:T(8,128)} %route.1), calls=%async_computation.1 | async-start | bytes 4194304 | tf_op jit(solution)/shard_map/all_to_all | solution.py:353
  186.5 49.2 %all-to-all-done.1.margins = f32[64,4,16,128]{3,2,1,0:T(8,128)S(1)} async-done(((f32[64,4,16,128]{3,2,1,0:T(8,128)}), f32[64,4,16,128]{3,2,1,0:T(8,128)S(1)}, u32[]{:S(2)}, u32[]{:S(2)}) %all-to-all-start.1) | async-done | bytes 2097184 | tf_op jit(solution)/shard_map/all_to_all | solution.py:353
  237.1 17.0 %finish.1 = f32[3,16,128,128]{3,2,1,0:T(8,128)} custom-call(s32[4]{0:T(128)} %dynamic-slice_reduce_fusion.1.glued, s32[4]{0:T(128)} %dynamic-slice_reduce_fusion.turned, bf16[256,256]{1,0:T(8,128)(2,1)} %constant.30.clone.pair, f32[128,192]{1,0:T(8,128)} %constant.32.clone.along, bf16[2,256,1024]{2,1,0:T(8,128)(2,1)} %constant.33.clone.spread, ...), custom_call_target="tpu_custom_call" | custom-call | flops 4294967296 | bytes 10485760 | tf_op jit(solution)/shard_map/finish/pallas_call | solution.py:293
  (33 shorter events, 7.0 us)
Async XLA Ops:
  0.0 15.6 %copy-start = (f32[1,16,128,128]{3,2,1,0:T(8,128)S(1)}, f32[1,16,128,128]{3,2,1,0:T(8,128)}, u32[]{:S(2)}) copy-start(f32[1,16,128,128]{3,2,1,0:T(8,128)} %param.12) | copy-start | bytes 3145732
  5.1 45.8 %copy-start.4 = (s32[64,4]{0,1:T(4,128)S(1)}, s32[64,4]{0,1:T(4,128)}, u32[]{:S(2)}) copy-start(s32[64,4]{0,1:T(4,128)} %param.14) | copy-start | bytes 3076
  5.1 46.5 %copy-start.1 = (f32[1,3,16,128,128]{4,3,2,1,0:T(8,128)S(1)}, f32[1,3,16,128,128]{4,3,2,1,0:T(8,128)}, u32[]{:S(2)}) copy-start(f32[1,3,16,128,128]{4,3,2,1,0:T(8,128)} %param.11) | copy-start | bytes 9437188
  5.1 25.5 %collective-permute-start.6 = (f32[15,128,128]{2,1,0:T(8,128)S(1)}, f32[15,128,128]{2,1,0:T(8,128)}, u32[]{:S(2)}, u32[]{:S(2)}) collective-permute-start(f32[15,128,128]{2,1,0:T(8,128)S(1)} %get-tuple-element.6), channel_id=1, source_target_pairs={{0,1},{1,2},{2,3},{4,5},{5,6},{6,7},{8,9},{9,10},{10,11},{12,13},{... | collective-permute-start | bytes 2949128 | tf_op jit(solution)/shard_map/ppermute | solution.py:329
  15.8 24.7 %collective-permute-start = (f32[15,128,128]{2,1,0:T(8,128)S(1)}, f32[15,128,128]{2,1,0:T(8,128)}, u32[]{:S(2)}, u32[]{:S(2)}) collective-permute-start(f32[15,128,128]{2,1,0:T(8,128)S(1)} %get-tuple-element.15), channel_id=1, source_target_pairs={{0,1},{1,2},{2,3},{4,5},{5,6},{6,7},{8,9},{9,10},{10,11},{12,13},{... | collective-permute-start | bytes 2949128 | tf_op jit(solution)/shard_map/ppermute | solution.py:329
  17.7 31.2 %collective-permute-start.1 = (f32[15,128,128]{2,1,0:T(8,128)S(1)}, f32[15,128,128]{2,1,0:T(8,128)}, u32[]{:S(2)}, u32[]{:S(2)}) collective-permute-start(f32[15,128,128]{2,1,0:T(8,128)S(1)} %get-tuple-element.14), channel_id=1, source_target_pairs={{1,0},{2,1},{3,2},{5,4},{6,5},{7,6},{9,8},{10,9},{11,10},{13,12},{... | collective-permute-start | bytes 2949128 | tf_op jit(solution)/shard_map/ppermute | solution.py:330
  21.1 36.9 %collective-permute-start.7 = (f32[15,128,128]{2,1,0:T(8,128)}, f32[15,128,128]{2,1,0:T(8,128)}, u32[]{:S(2)}, u32[]{:S(2)}) collective-permute-start(f32[15,128,128]{2,1,0:T(8,128)} %get-tuple-element.5), channel_id=1, source_target_pairs={{1,0},{2,1},{3,2},{5,4},{6,5},{7,6},{9,8},{10,9},{11,10},{13,12},{... | collective-permute-start | bytes 2949128 | tf_op jit(solution)/shard_map/ppermute | solution.py:330
  23.0 40.4 %collective-permute-start.4 = (f32[15,128,128]{2,1,0:T(8,128)}, f32[15,128,128]{2,1,0:T(8,128)}, u32[]{:S(2)}, u32[]{:S(2)}) collective-permute-start(f32[15,128,128]{2,1,0:T(8,128)} %get-tuple-element.8), channel_id=1, source_target_pairs={{0,1},{1,2},{2,3},{4,5},{5,6},{6,7},{8,9},{9,10},{10,11},{12,13},{... | collective-permute-start | bytes 2949128 | tf_op jit(solution)/shard_map/ppermute | solution.py:329
  30.6 38.8 %collective-permute-start.5 = (f32[15,128,128]{2,1,0:T(8,128)}, f32[15,128,128]{2,1,0:T(8,128)}, u32[]{:S(2)}, u32[]{:S(2)}) collective-permute-start(f32[15,128,128]{2,1,0:T(8,128)} %get-tuple-element.7), channel_id=1, source_target_pairs={{1,0},{2,1},{3,2},{5,4},{6,5},{7,6},{9,8},{10,9},{11,10},{13,12},{... | collective-permute-start | bytes 2949128 | tf_op jit(solution)/shard_map/ppermute | solution.py:330
  40.5 34.4 %collective-permute-start.2 = (f32[15,128,128]{2,1,0:T(8,128)}, f32[15,128,128]{2,1,0:T(8,128)}, u32[]{:S(2)}, u32[]{:S(2)}) collective-permute-start(f32[15,128,128]{2,1,0:T(8,128)} %get-tuple-element.10), channel_id=1, source_target_pairs={{0,1},{1,2},{2,3},{4,5},{5,6},{6,7},{8,9},{9,10},{10,11},{12,13},{... | collective-permute-start | bytes 2949128 | tf_op jit(solution)/shard_map/ppermute | solution.py:329
  49.0 61.5 %collective-permute-start.3 = (f32[15,128,128]{2,1,0:T(8,128)}, f32[15,128,128]{2,1,0:T(8,128)}, u32[]{:S(2)}, u32[]{:S(2)}) collective-permute-start(f32[15,128,128]{2,1,0:T(8,128)} %get-tuple-element.9), channel_id=1, source_target_pairs={{1,0},{2,1},{3,2},{5,4},{6,5},{7,6},{9,8},{10,9},{11,10},{13,12},{... | collective-permute-start | bytes 2949128 | tf_op jit(solution)/shard_map/ppermute | solution.py:330
  121.4 10.4 %copy-start.6 = (s32[64,4]{0,1:T(4,128)S(1)}, s32[64,4]{0,1:T(4,128)}, u32[]{:S(2)}) copy-start(s32[64,4]{0,1:T(4,128)} %param.15) | copy-start | bytes 3076
  121.4 11.4 %copy-start.5 = (s32[64,4]{0,1:T(4,128)S(1)}, s32[64,4]{0,1:T(4,128)}, u32[]{:S(2)}) copy-start(s32[64,4]{0,1:T(4,128)} %param.13) | copy-start | bytes 3076
  121.4 53.1 %all-to-all-start = ((f32[64,4,16,128]{3,2,1,0:T(8,128)}), f32[64,4,16,128]{3,2,1,0:T(8,128)S(1)}, u32[]{:S(2)}, u32[]{:S(2)}) async-start(f32[64,4,16,128]{3,2,1,0:T(8,128)} %pack.1), calls=%async_computation | async-start | bytes 4194304 | tf_op jit(solution)/shard_map/all_to_all | solution.py:351
  174.5 1.3 copy-start.2
  181.0 54.7 %all-to-all-start.1 = ((f32[64,4,16,128]{3,2,1,0:T(8,128)}), f32[64,4,16,128]{3,2,1,0:T(8,128)S(1)}, u32[]{:S(2)}, u32[]{:S(2)}) async-start(f32[64,4,16,128]{3,2,1,0:T(8,128)} %route.1), calls=%async_computation.1 | async-start | bytes 4194304 | tf_op jit(solution)/shard_map/all_to_all | solution.py:353
  235.7 1.4 copy-start.3
where the time goes:
time: 255 us; the launch traced here: 254 us
  waiting for transfers between devices  139 us (55%)
  starting transfers between devices  52.6 us (21%)
  Pallas kernels  48.5 us (19%)
  local copies, waits for them, and re-layouts  13.8 us (5%)
    all_to_all x1, waiting for transfers between devices, per_device(): lax.all_to_all(picked, 'tile', split_axis=0, concat_axis=0, tiled=True)  49.2 us
    ppermute x4, waiting for transfers between devices, with_halo(): above = lax.ppermute(levels[:-1], 'slab', DOWN)  41.6 us
    all_to_all x1, waiting for transfers between devices, per_device(): lax.all_to_all(strips, 'tile', split_axis=0, concat_axis=0, tiled=True)  40.2 us
    ppermute x4, starting transfers between devices, with_halo(): below = lax.ppermute(levels[1:], 'slab', UP)  28.4 us
    pallas_call x4, Pallas kernels, radial(): pl.pallas_call(functools.partial(radial_kernel, weighted), grid=(SIDE //...  20.9 us
    pallas_call x1, Pallas kernels, finish(): pl.pallas_call(finish_kernel, grid=(4,), in_specs=[SMEM, SMEM] + [pl.Bloc...  17 us
    all_to_all x1, starting transfers between devices, per_device(): lax.all_to_all(strips, 'tile', split_axis=0, concat_axis=0, tiled=True)  10.4 us
    ppermute x4, starting transfers between devices, with_halo(): above = lax.ppermute(levels[:-1], 'slab', DOWN)  9.13 us
  transfers between devices with their start and end apart: 10, of which 5 were waited for; matrix products, arithmetic and copies ran while one was open for 2% of the time, Pallas kernels for 6%

commit v1 on v0

v1 whole, which is shorter than its diff:
```python
import functools
import math

import jax
import jax.numpy as jnp
import numpy as np
from jax import lax
from jax.experimental import pallas as pl
from jax.experimental.pallas import tpu as pltpu
from jax.sharding import PartitionSpec as P


SIDE = 128
HALF = 15
DEEP = 16
OWN = 16
SPAN = 2 * HALF + OWN
F32 = jnp.float32
BF16 = jnp.bfloat16

ROOM = pltpu.CompilerParams(vmem_limit_bytes=24 << 20)
TAPS = [float(np.float32(math.exp(-k * k / 50.0))) for k in range(HALF + 1)]


def tap(offset):
    offset = np.abs(np.asarray(offset))
    return np.where(offset <= HALF, np.exp(-(offset.astype(np.float64) ** 2) / 50.0), 0.0).astype(np.float32)


def halves(values):
    high = values.astype(BF16)
    low = (values - high.astype(np.float32)).astype(BF16)
    return high, low


def constants():
    cell = np.arange(SIDE)
    deep = np.arange(DEEP)
    live = (deep < HALF)[:, None]
    square = tap(cell[:, None] - cell[None, :])
    high, low = halves(square)
    pair = np.block([[high, low], [high, np.zeros_like(low)]])
    near = tap(cell[None, :] + deep[:, None] + 1) * live
    far = tap(SIDE - cell[None, :] + deep[:, None]) * live
    pick_west = (cell[None, :] == deep[:, None]).astype(np.float32) * live
    pick_east = (cell[None, :] == SIDE - 1 - deep[:, None]).astype(np.float32) * live
    sum_west = tap(cell[None, :] - deep[:, None]) * live
    sum_east = tap(cell[None, :] - (SIDE - 1 - deep[:, None])) * live
    picks = np.stack([pick_west, pick_east, sum_west, sum_east])
    back = tap(deep[:, None] + deep[None, :] + 1) * live * live.T
    south_own = near.T.astype(np.float64) @ back
    north_own = (far.T.astype(np.float64) @ back)[:, ::-1]
    along = np.concatenate([square, south_own, north_own], axis=1).astype(np.float32)
    ahead_high, ahead_low = halves(np.concatenate([near.T, far.T], axis=1))
    eye = np.eye(4, dtype=np.float32)
    spread_high, spread_low = halves(np.concatenate([np.kron(eye, near), np.kron(eye, far)], axis=0))
    corner = np.kron(eye, np.concatenate([near, far], axis=0))
    ends = np.concatenate([pick_west, pick_east], axis=0)
    return dict(
        pair=pair,
        picks=picks,
        along=along,
        square=np.stack([high, low]),
        ahead=np.concatenate([ahead_high, ahead_high, ahead_low], axis=1),
        spread=np.concatenate([spread_high, spread_high, spread_low], axis=0),
        corner=np.stack(halves(corner)),
        ends=ends.astype(BF16),
    )


def split(values):
    high = values.astype(BF16)
    return high, (values - high.astype(F32)).astype(BF16)


def dot(left, right):
    return jnp.dot(left, right, preferred_element_type=F32)


def dot_t(left, right):
    return lax.dot_general(left, right, (((1,), (1,)), ((), ())), preferred_element_type=F32)


def through(rows, pair):
    high, low = split(rows)
    both = dot(jnp.concatenate([high, low], axis=1), pair)
    return both[:, :SIDE] + both[:, SIDE:]


VMEM = pl.BlockSpec(memory_space=pltpu.VMEM)
SMEM = pl.BlockSpec(memory_space=pltpu.SMEM)


PAIRS = 48
RIM = 2 * DEEP + PAIRS
QUARTER = SIDE // 4
UPPER = DEEP + PAIRS


def lanes(shape):
    return lax.broadcasted_iota(jnp.int32, shape, len(shape) - 1)


def rolled(x, amount):
    return pltpu.roll(x, amount, x.ndim - 1)


def two(first, second):
    return jnp.where(lanes(first.shape) < SIDE // 2, first, second)


def rim_pairs(first, second):
    return two(rolled(first, QUARTER), rolled(second, 3 * QUARTER))


def core_pairs(first, second):
    return two(rolled(first, 3 * QUARTER), rolled(second, QUARTER))


def unpair(rim, core):
    edge = lanes(rim.shape)
    edge = (edge < QUARTER) | (edge >= 3 * QUARTER)
    inside = (rolled(core, QUARTER), rolled(core, 3 * QUARTER)) if core is not None else (0.0, 0.0)
    return jnp.where(edge, rolled(rim, 3 * QUARTER), inside[0]), jnp.where(edge, rolled(rim, QUARTER), inside[1])


def levels_out(l, value, at, own, up, down):
    own[l, at, :] = value
    if l > 0:
        up[l - 1, at, :] = value
    if l < OWN - 1:
        down[l, at, :] = value


def rim_kernel(weighted, *refs):
    outs = refs[2 if weighted else 1 :]
    for l in range(OWN):

        def rows(start, count):
            x = refs[0][0, l, start : start + count, :]
            return x * refs[1][0, l, start : start + count, :] if weighted else x

        levels_out(l, rows(0, DEEP), slice(0, DEEP), *outs)
        levels_out(l, rows(SIDE - DEEP, DEEP), slice(DEEP, 2 * DEEP), *outs)
        levels_out(l, rim_pairs(rows(DEEP, PAIRS), rows(UPPER, PAIRS)), slice(2 * DEEP, RIM), *outs)


def rim_of(kernels, volume, field):
    arrays = [volume] if field is None else [kernels, volume]
    spec = [pl.BlockSpec((1, OWN, SIDE, SIDE), lambda i: (0, 0, 0, 0))]
    if field is not None:
        spec = [pl.BlockSpec((1, OWN, SIDE, SIDE), lambda i: (field, 0, 0, 0))] + spec
    shapes = [jax.ShapeDtypeStruct((count, RIM, SIDE), F32) for count in (OWN, OWN - 1, OWN - 1)]
    return pl.pallas_call(
        functools.partial(rim_kernel, field is not None),
        grid=(1,),
        in_specs=spec,
        out_specs=[pl.BlockSpec(x.shape, lambda i: (0, 0, 0)) for x in shapes],
        out_shape=shapes,
        name="rim",
        compiler_params=ROOM,
        cost_estimate=pl.CostEstimate(flops=1 << 20, bytes_accessed=4 << 20, transcendentals=0),
    )(*arrays)


def core_kernel(kernels, volume, own, up, down):
    field = jnp.full((PAIRS, SIDE), pl.program_id(0), jnp.int32)
    for l in range(OWN):
        parts = []
        for start in (DEEP, UPPER):
            w = volume[l, start : start + PAIRS, :]
            parts.append(jnp.where(field == 0, w, w * kernels[0, l, start : start + PAIRS, :]))
        levels_out(l, core_pairs(*parts), slice(0, PAIRS), own.at[0], up.at[0], down.at[0])


def core_of(kernels, volume):
    counts = (OWN, OWN - 1, OWN - 1)
    return pl.pallas_call(
        core_kernel,
        grid=(4,),
        in_specs=[
            pl.BlockSpec((1, OWN, SIDE, SIDE), lambda i: (jnp.maximum(i - 1, 0), 0, 0, 0)),
            pl.BlockSpec((OWN, SIDE, SIDE), lambda i: (0, 0, 0)),
        ],
        out_specs=[pl.BlockSpec((1, c, PAIRS, SIDE), lambda i: (i, 0, 0, 0)) for c in counts],
        out_shape=[jax.ShapeDtypeStruct((4, c, PAIRS, SIDE), F32) for c in counts],
        name="core",
        compiler_params=ROOM,
        cost_estimate=pl.CostEstimate(flops=1 << 20, bytes_accessed=10 << 20, transcendentals=0),
    )(kernels, volume)


def radial_kernel(below, own, above, out):
    parts = (below, own, above)

    def tile(i, carry):
        at = pl.ds(pl.multiple_of(i * 8, 8), 8)

        def level(j):
            part, k = (0, j) if j < HALF else (1, j - HALF) if j < HALF + OWN else (2, j - HALF - OWN)
            return parts[part][0, k, at, :]

        x = [level(j) for j in range(SPAN)]
        for m in range(OWN):
            c = m + HALF
            total = TAPS[0] * x[c]
            for k in range(1, HALF + 1):
                total = total + TAPS[k] * (x[c - k] + x[c + k])
            out[0, m, at, :] = total
        return carry

    lax.fori_loop(0, out.shape[2] // 8, tile, 0)


def radial(below, own, above):
    count, _, rows, _ = own.shape
    block = rows // 2
    return pl.pallas_call(
        radial_kernel,
        grid=(count, rows // block),
        in_specs=[pl.BlockSpec((1, a.shape[1], block, SIDE), lambda f, i: (f, 0, i, 0)) for a in (below, own, above)],
        out_specs=pl.BlockSpec((1, OWN, block, SIDE), lambda f, i: (f, 0, i, 0)),
        out_shape=jax.ShapeDtypeStruct(own.shape, F32),
        name="radial",
        compiler_params=ROOM,
        cost_estimate=pl.CostEstimate(
            flops=count * OWN * SPAN * rows * SIDE * 2, bytes_accessed=count * 62 * rows * 512, transcendentals=0
        ),
    )(below, own, above)


def pack_kernel(field_count, glued, pair, picks, *refs):
    fields = refs[:field_count]
    out, edge, rows = refs[field_count:]

    def choose(side):
        raw = jnp.where(glued[side] < 2, 1.0, 0.0).astype(F32)
        return picks[side] * raw + picks[side + 2] * (1.0 - raw)

    left_high, left_low = split(jnp.concatenate([choose(0), choose(1)], axis=0))
    left = jnp.concatenate([left_high, left_low], axis=0)
    for f in range(field_count):
        rim = fields[f]
        mine = pl.ds(f * OWN, OWN)
        for q in range(OWN):
            base = q * SIDE
            rows[base : base + DEEP, :] = rim[q, :DEEP, :]
            rows[base + SIDE - DEEP : base + SIDE, :] = rim[q, DEEP : 2 * DEEP, :]
            first, second = unpair(rim[q, 2 * DEEP :, :], None)
            rows[base + DEEP : base + UPPER, :] = first
            rows[base + UPPER : base + SIDE - DEEP, :] = second
        for d in range(DEEP):
            edge[pl.ds(d, OWN, stride=DEEP), :] = rows[pl.ds(d, OWN, stride=SIDE), :]
            edge[pl.ds(OWN * DEEP + d, OWN, stride=DEEP), :] = rows[pl.ds(SIDE - 1 - d, OWN, stride=SIDE), :]
        raw = edge[...]
        across = through(raw, pair[...])
        for side in (2, 3):
            at = slice((side - 2) * OWN * DEEP, (side - 1) * OWN * DEEP)
            strip = jnp.where(glued[side] < 2, raw[at], across[at])
            out[mine, side, :, :] = strip.reshape(OWN, DEEP, SIDE)
        high, low = split(rows[...])
        both = dot_t(left, high)
        strips = both[: 2 * DEEP] + both[2 * DEEP :] + dot_t(left_high, low)
        for q in range(OWN):
            plane = strips[:, q * SIDE : (q + 1) * SIDE]
            out[f * OWN + q, 0, :, :] = plane[:DEEP]
            out[f * OWN + q, 1, :, :] = plane[DEEP:]


def pack(rims, glued, const):
    count = len(rims)
    return pl.pallas_call(
        functools.partial(pack_kernel, count),
        in_specs=[SMEM] + [VMEM] * (2 + count),
        out_specs=VMEM,
        out_shape=jax.ShapeDtypeStruct((count * OWN, 4, DEEP, SIDE), F32),
        scratch_shapes=[pltpu.VMEM((2 * OWN * DEEP, SIDE), F32), pltpu.VMEM((OWN * SIDE, SIDE), F32)],
        name="pack",
        compiler_params=ROOM,
        cost_estimate=pl.CostEstimate(flops=1 << 29, bytes_accessed=6 << 20, transcendentals=0),
    )(glued, const["pair"], const["picks"], *rims)


def route_kernel(source, fix, ends, corner, flipped, strips, out, patch):
    tiles = out.shape[0]
    group = 4

    def move(i, carry):
        for j in range(8):
            e = i * 8 + j
            t, s = i * 2 + j // 4, j % 4
            out[t, s, :, :] = strips[source[e], :, :]
        return carry

    lax.fori_loop(0, tiles // 2, move, 0)
    margins = out[:, 0:2, :, :].reshape(tiles * 2 * DEEP, SIDE)
    high, low = split(margins)
    seen = dot_t(ends[...], high) + dot_t(ends[...], low)
    first, last = seen[:DEEP], seen[DEEP:]
    swap = flipped[...] > 0.5
    turned = jnp.concatenate([jnp.where(swap, last, first), jnp.where(swap, first, last)], axis=0)
    high, low = split(turned)
    for g in range(tiles // group):
        at = slice(g * SIDE, (g + 1) * SIDE)
        added = dot(high[:, at], corner[0]) + dot(high[:, at], corner[1]) + dot(low[:, at], corner[0])
        for j in range(group):
            block = added[:, j * SIDE : (j + 1) * SIDE]
            patch[(g * group + j) * 2] = block[:DEEP]
            patch[(g * group + j) * 2 + 1] = block[DEEP:]
    patch[tiles * 2] = jnp.zeros((DEEP, SIDE), F32)

    def mend(i, carry):
        for j in range(4):
            t, s = i * 2 + j // 2, 2 + j % 2
            out[t, s, :, :] = out[t, s, :, :] + patch[fix[i * 4 + j], :, :]
        return carry

    lax.fori_loop(0, tiles // 2, mend, 0)


def route(strips, tables, const):
    tiles = strips.shape[0]
    source, fix, flipped = tables
    return pl.pallas_call(
        route_kernel,
        in_specs=[SMEM, SMEM] + [VMEM] * 4,
        out_specs=VMEM,
        out_shape=jax.ShapeDtypeStruct((tiles, 4, DEEP, SIDE), F32),
        scratch_shapes=[pltpu.VMEM((tiles * 2 + 1, DEEP, SIDE), F32)],
        name="route",
        compiler_params=ROOM,
        cost_estimate=pl.CostEstimate(flops=1 << 28, bytes_accessed=4 << 20, transcendentals=0),
    )(source, fix, const["ends"], const["corner"], flipped, strips.reshape(tiles * 4, DEEP, SIDE))


def base_kernel(glued, pair, along, core, *refs):
    rims = refs[:4]
    out, rows, across = refs[4:]
    f = pl.program_id(0)
    lane = lanes((SIDE, along.shape[1]))
    south = jnp.where(glued[2] < 2, 1.0, 0.0).astype(F32)
    north = jnp.where(glued[3] < 2, 1.0, 0.0).astype(F32)
    scale = jnp.where(lane < SIDE, 1.0, jnp.where(lane < SIDE + DEEP, south, north))
    left_high, left_low = split(along[...] * scale)
    left = jnp.concatenate([left_high, left_low], axis=0)
    for k in range(4):

        @pl.when(f == k)
        def _():
            for q in range(OWN):
                base = q * SIDE
                rows[base : base + DEEP, :] = rims[k][q, :DEEP, :]
                rows[base + SIDE - DEEP : base + SIDE, :] = rims[k][q, DEEP : 2 * DEEP, :]
                first, second = unpair(rims[k][q, 2 * DEEP :, :], core[0, q])
                rows[base + DEEP : base + UPPER, :] = first
                rows[base + UPPER : base + SIDE - DEEP, :] = second

    across[...] = through(rows[...], pair[...])

    def column(q):
        base = q * SIDE
        own = [rows[base : base + DEEP, :], rows[base + SIDE - DEEP : base + SIDE, :]]
        return jnp.concatenate([across[base : base + SIDE, :]] + own, axis=0)

    for q in range(0, OWN, 2):
        high, low = split(jnp.concatenate([column(q), column(q + 1)], axis=1))
        both = dot(left, high)
        total = both[:SIDE] + both[SIDE:] + dot(left_high, low)
        out[0, q] = total[:, :SIDE]
        out[0, q + 1] = total[:, SIDE:]


def base_lateral(rims, core, glued, const):
    plane = (1, OWN, SIDE, SIDE)
    return pl.pallas_call(
        base_kernel,
        grid=(4,),
        in_specs=[
            SMEM,
            pl.BlockSpec(const["pair"].shape, lambda i: (0, 0)),
            pl.BlockSpec(const["along"].shape, lambda i: (0, 0)),
            pl.BlockSpec((1, OWN, PAIRS, SIDE), lambda i: (i, 0, 0, 0)),
        ]
        + [pl.BlockSpec((OWN, RIM, SIDE), lambda i: (0, 0, 0))] * 4,
        out_specs=pl.BlockSpec(plane, lambda i: (i, 0, 0, 0)),
        out_shape=jax.ShapeDtypeStruct((4,) + plane[1:], F32),
        scratch_shapes=[pltpu.VMEM((OWN * SIDE, SIDE), F32)] * 2,
        name="base",
        compiler_params=ROOM,
        cost_estimate=pl.CostEstimate(flops=1 << 32, bytes_accessed=9 << 20, transcendentals=0),
    )(glued, const["pair"], const["along"], core, *rims)


def turn(code):
    row = lax.broadcasted_iota(jnp.int32, (SIDE, SIDE), 0)
    col = lax.broadcasted_iota(jnp.int32, (SIDE, SIDE), 1)
    return jnp.where(col == jnp.where(code == 1, SIDE - 1 - row, row), 1.0, 0.0).astype(BF16)


def finish_kernel(turned, square, ahead, spread, margins, base, out, below, ways):
    f = pl.program_id(0)
    size = OWN * DEEP

    @pl.when(f == 0)
    def _():
        for side in range(4):
            way = turn(turned[side])
            if side < 2:
                ways[side, 0] = dot(square[0], way).astype(BF16)
                ways[side, 1] = dot(square[1], way).astype(BF16)
            else:
                ways[side, 0] = way

    def margin(side):
        return split(margins[:, side, :, :].reshape(size, SIDE))

    sides = []
    for side in (0, 1):
        high, low = margin(side)
        both = dot_t(ways[side].reshape(2 * SIDE, SIDE), high)
        sides.append(both[:SIDE] + both[SIDE:] + dot_t(ways[side, 0], low))
    rows = []
    for side in (2, 3):
        high, low = margin(side)
        way = ways[side, 0]
        rows.append((dot(high, way) + dot(low, way)).reshape(OWN, DEEP, SIDE))
    planes = 4
    for g in range(OWN // planes):
        at = slice(g * planes * DEEP, (g + 1) * planes * DEEP)
        high, low = split(jnp.concatenate([sides[0][:, at], sides[1][:, at]], axis=1))
        left = jnp.concatenate([high, low], axis=1)
        for j in range(0, planes, 2):
            to = slice(j * SIDE, (j + 2) * SIDE)
            total = dot(left, spread[: 2 * SIDE, to]) + dot(high, spread[2 * SIDE :, to])
            q = g * planes + j
            pairs = [jnp.concatenate([rows[0][k], rows[1][k]], axis=0) for k in (q, q + 1)]
            right, rest = split(jnp.concatenate(pairs, axis=1))
            total = total + dot(ahead[...], jnp.concatenate([right, rest, right], axis=0))
            for k in range(2):
                plane = total[:, k * SIDE : (k + 1) * SIDE] + base[0, q + k]

                @pl.when(f == 0)
                def _():
                    below[q + k] = 1.0 / plane

                @pl.when(f > 0)
                def _():
                    out[0, q + k] = plane * below[q + k]


def finish(base, margins, turned, const):
    plane = (1, OWN, SIDE, SIDE)
    return pl.pallas_call(
        finish_kernel,
        grid=(4,),
        in_specs=[
            SMEM,
            pl.BlockSpec(const["square"].shape, lambda i: (0, 0, 0)),
            pl.BlockSpec(const["ahead"].shape, lambda i: (0, 0)),
            pl.BlockSpec(const["spread"].shape, lambda i: (0, 0)),
            pl.BlockSpec((OWN, 4, DEEP, SIDE), lambda i: (i, 0, 0, 0)),
            pl.BlockSpec(plane, lambda i: (i, 0, 0, 0)),
        ],
        out_specs=pl.BlockSpec(plane, lambda i: (jnp.maximum(i - 1, 0), 0, 0, 0)),
        out_shape=jax.ShapeDtypeStruct((3,) + plane[1:], F32),
        scratch_shapes=[pltpu.VMEM(plane[1:], F32), pltpu.VMEM((4, 2, SIDE, SIDE), BF16)],
        name="finish",
        compiler_params=ROOM,
        cost_estimate=pl.CostEstimate(flops=1 << 32, bytes_accessed=9 << 20, transcendentals=0),
    )(turned, const["square"], const["ahead"], const["spread"], margins, base)


UP = [(0, 1), (1, 2), (2, 3)]
DOWN = [(1, 0), (2, 1), (3, 2)]


def with_halo(own, up, down):
    return lax.ppermute(up, "slab", UP), own, lax.ppermute(down, "slab", DOWN)


def per_device(kernels, volume, neighbours, glued_sides, reversals):
    const = {k: jnp.asarray(v) for k, v in constants().items()}
    tile = lax.axis_index("tile")
    glued = glued_sides[tile]
    turned = reversals[tile]
    tiles = neighbours.shape[0]
    source = (neighbours * 4 + glued_sides).reshape(-1)
    ahead = glued_sides[:, 2:]
    fix = jnp.where(ahead >= 2, neighbours[:, 2:] * 2 + ahead - 2, tiles * 2).reshape(-1)
    flipped = jnp.repeat(reversals[:, :2].astype(F32).reshape(-1), DEEP)[None, :]
    tables = (source, fix, flipped)

    def to_all(x):
        return lax.all_to_all(x, "tile", split_axis=0, concat_axis=0, tiled=True)

    rims = []
    for f in (None, 0, 1, 2):
        parts = rim_of(kernels[0], volume, f)
        rims.append(radial(*[x[None] for x in with_halo(*parts)])[0])
    own, up, down = core_of(kernels[0], volume[0])
    below, own, above = with_halo(own, up, down)
    routed_in = to_all(pack(rims, glued, const))
    routed = route(routed_in, tables, const)
    margins = to_all(routed)
    base = base_lateral(rims, radial(below, own, above), glued, const)
    return finish(base, margins, turned, const)[None]


def solution(mesh):
    placed = (P("tile", None, "slab", None, None), P("tile", "slab", None, None), P(), P(), P())
    return jax.shard_map(
        per_device,
        mesh=mesh,
        in_specs=placed,
        out_specs=P("tile", None, "slab", None, None),
        check_vma=False,
    )
```

time: 255 us -> 229 us (0.90)
  waiting for transfers between devices: 139 us -> 94.3 us
  starting transfers between devices: 52.6 us -> 76.1 us
  Pallas kernels: 48.5 us -> 42.2 us
    all_to_all x2, waiting for transfers between devices: 89.4 us -> 30.5 us  [to_all(): return lax.all_to_all(x, 'tile', split_axis=0, concat_axis=0, tiled=True)]
    ppermute x8 -> x10, waiting for transfers between devices: 49.5 us -> 63.8 us  [with_halo(): return (lax.ppermute(up, 'slab', UP), own, lax.ppermute(down, 'slab', DOWN))]
    ppermute x8 -> x10, starting transfers between devices: 37.6 us -> 51.1 us  [with_halo(): return (lax.ppermute(up, 'slab', UP), own, lax.ppermute(down, 'slab', DOWN))]
    unnamed x14 -> x60, local copies, waits for them, and re-layouts: 2.69 us -> 13.4 us
    all_to_all x2, starting transfers between devices: 15.1 us -> 25 us  [to_all(): return lax.all_to_all(x, 'tile', split_axis=0, concat_axis=0, tiled=True)]
    slice x2 -> x0, local copies, waits for them, and re-layouts: 5.32 us -> none  [with_halo(): above = lax.ppermute(levels[:-1], 'slab', DOWN)]
    pallas_call x1, Pallas kernels: 5.16 us -> 2.55 us  [route(): pl.pallas_call(route_kernel, in_specs=[SMEM, SMEM] + [VMEM] * 4, out_spec...]
    pallas_call x5 -> x12, Pallas kernels: 37.8 us -> 35.4 us  [the longest x1 12.2 us: finish(): pl.pallas_call(finish_kernel, grid=(4,), in_specs=[SMEM, pl.BlockSpec(con...]
  transfers between devices with their start and end apart: 10 -> 12, of which waited for: 5 -> 7; matrix products, arithmetic and copies ran while one was open for 2% -> 1% of each run, Pallas kernels for 6% -> 9%
where the time goes in v1:
time: 229 us; the launch traced here: 228 us
  waiting for transfers between devices  94.3 us (41%)
  starting transfers between devices  76.1 us (33%)
  Pallas kernels  42.2 us (18%)
  local copies, waits for them, and re-layouts  14.7 us (6%)
    ppermute x10, waiting for transfers between devices, with_halo(): return (lax.ppermute(up, 'slab', UP), own, lax.ppermute(down, 'slab', DOWN))  63.8 us
    ppermute x10, starting transfers between devices, with_halo(): return (lax.ppermute(up, 'slab', UP), own, lax.ppermute(down, 'slab', DOWN))  51.1 us
    all_to_all x2, waiting for transfers between devices, to_all(): return lax.all_to_all(x, 'tile', split_axis=0, concat_axis=0, tiled=True)  30.5 us
    all_to_all x2, starting transfers between devices, to_all(): return lax.all_to_all(x, 'tile', split_axis=0, concat_axis=0, tiled=True)  25 us
    unnamed x60, local copies, waits for them, and re-layouts  13.4 us
    pallas_call x1, Pallas kernels, finish(): pl.pallas_call(finish_kernel, grid=(4,), in_specs=[SMEM, pl.BlockSpec(con...  12.2 us
    pallas_call x5, Pallas kernels, radial(): pl.pallas_call(radial_kernel, grid=(count, rows // block), in_specs=[pl.B...  11.3 us
    pallas_call x1, Pallas kernels, base_lateral(): pl.pallas_call(base_kernel, grid=(4,), in_specs=[SMEM, pl.BlockSpec(const...  6.72 us
  transfers between devices with their start and end apart: 12, of which 7 were waited for; matrix products, arithmetic and copies ran while one was open for 1% of the time, Pallas kernels for 9%

profile of v1, /device:TPU:1, one launch (start us, length us, event | category | flops | bytes accessed | tf_op | source)
XLA Modules:
  0.0 227.8 jit_solution(1247752882153748318)
XLA Ops:
  3.4 5.1 %collective-permute-start.5 = (f32[15,80,128]{2,1,0:T(8,128)S(1)}, f32[15,80,128]{2,1,0:T(8,128)S(1)}, u32[]{:S(2)}, u32[]{:S(2)}) collective-permute-start(f32[15,80,128]{2,1,0:T(8,128)S(1)} %get-tuple-element.28), channel_id=1, source_target_pairs={{1,0},{2,1},{3,2},{5,4},{6,5},{7,6},{9,8},{10,9},{11,10},{13,12},{... | collective-permute-start | bytes 1843208 | tf_op jit(solution)/shard_map/ppermute | solution.py:478
  8.5 7.0 %collective-permute-start.4 = (f32[15,80,128]{2,1,0:T(8,128)S(1)}, f32[15,80,128]{2,1,0:T(8,128)S(1)}, u32[]{:S(2)}, u32[]{:S(2)}) collective-permute-start(f32[15,80,128]{2,1,0:T(8,128)S(1)} %get-tuple-element.26), channel_id=1, source_target_pairs={{0,1},{1,2},{2,3},{4,5},{5,6},{6,7},{8,9},{9,10},{10,11},{12,13},{... | collective-permute-start | bytes 1843208 | tf_op jit(solution)/shard_map/ppermute | solution.py:478
  16.6 2.4 %collective-permute-start.6 = (f32[15,80,128]{2,1,0:T(8,128)S(1)}, f32[15,80,128]{2,1,0:T(8,128)S(1)}, u32[]{:S(2)}, u32[]{:S(2)}) collective-permute-start(f32[15,80,128]{2,1,0:T(8,128)S(1)} %get-tuple-element.29), channel_id=1, source_target_pairs={{0,1},{1,2},{2,3},{4,5},{5,6},{6,7},{8,9},{9,10},{10,11},{12,13},{... | collective-permute-start | bytes 1843208 | tf_op jit(solution)/shard_map/ppermute | solution.py:478
  22.3 7.5 %collective-permute-start.2 = (f32[15,80,128]{2,1,0:T(8,128)}, f32[15,80,128]{2,1,0:T(8,128)}, u32[]{:S(2)}, u32[]{:S(2)}) collective-permute-start(f32[15,80,128]{2,1,0:T(8,128)} %get-tuple-element.23), channel_id=1, source_target_pairs={{0,1},{1,2},{2,3},{4,5},{5,6},{6,7},{8,9},{9,10},{10,11},{12,13},{... | collective-permute-start | bytes 1843208 | tf_op jit(solution)/shard_map/ppermute | solution.py:478
  35.6 8.5 %collective-permute-start = (f32[15,80,128]{2,1,0:T(8,128)}, f32[15,80,128]{2,1,0:T(8,128)}, u32[]{:S(2)}, u32[]{:S(2)}) collective-permute-start(f32[15,80,128]{2,1,0:T(8,128)} %get-tuple-element.20), channel_id=1, source_target_pairs={{0,1},{1,2},{2,3},{4,5},{5,6},{6,7},{8,9},{9,10},{10,11},{12,13},{... | collective-permute-start | bytes 1843208 | tf_op jit(solution)/shard_map/ppermute | solution.py:478
  49.5 2.3 %radial.8 = f32[1,16,80,128]{3,2,1,0:T(8,128)S(1)} custom-call(f32[1,15,80,128]{3,2,1,0:T(8,128)S(1)} %bitcast.40, f32[1,16,80,128]{3,2,1,0:T(8,128)S(1)} %bitcast.36, f32[1,15,80,128]{3,2,1,0:T(8,128)} %bitcast.15.above), custom_call_target="tpu_custom_call" | custom-call | flops 15073280 | bytes 2539520 | tf_op jit(solution)/shard_map/radial/pallas_call | solution.py:218
  51.8 3.4 %collective-permute-done.3 = f32[15,80,128]{2,1,0:T(8,128)} collective-permute-done((f32[15,80,128]{2,1,0:T(8,128)}, f32[15,80,128]{2,1,0:T(8,128)}, u32[]{:S(2)}, u32[]{:S(2)}) %collective-permute-start.3) | collective-permute-done | bytes 614432 | tf_op jit(solution)/shard_map/ppermute | solution.py:478
  55.2 2.2 radial.6
  57.5 2.6 %collective-permute-done = f32[15,80,128]{2,1,0:T(8,128)} collective-permute-done((f32[15,80,128]{2,1,0:T(8,128)}, f32[15,80,128]{2,1,0:T(8,128)}, u32[]{:S(2)}, u32[]{:S(2)}) %collective-permute-start) | collective-permute-done | bytes 614432 | tf_op jit(solution)/shard_map/ppermute | solution.py:478
  60.1 2.9 %collective-permute-done.1 = f32[15,80,128]{2,1,0:T(8,128)} collective-permute-done((f32[15,80,128]{2,1,0:T(8,128)}, f32[15,80,128]{2,1,0:T(8,128)}, u32[]{:S(2)}, u32[]{:S(2)}) %collective-permute-start.1) | collective-permute-done | bytes 614432 | tf_op jit(solution)/shard_map/ppermute | solution.py:478
  63.0 2.2 radial.5
  65.3 4.3 %pack.1 = f32[64,4,16,128]{3,2,1,0:T(8,128)} custom-call(s32[4]{0:T(128)S(1)} %dynamic-slice_reduce_fusion.glued, bf16[256,256]{1,0:T(8,128)(2,1)S(1)} %copy-done.18, f32[4,16,128]{2,1,0:T(8,128)S(1)} %copy-done.19, f32[16,80,128]{2,1,0:T(8,128)S(1)} %bitcast.32, f32[16,80,128]{2,1,0:T(8,128)S(1)} %bitcast.30, f32[16,80,128]{2,1,0:T(8,128)S(1)} %bitcast.26, ...), custom_call_target="tpu_custom_call" | custom-call | flops 536870912 | bytes 6291456 | tf_op jit(solution)/shard_map/pack/pallas_call | solution.py:272
  70.4 17.7 %all-to-all-start = ((f32[64,4,16,128]{3,2,1,0:T(8,128)}), f32[64,4,16,128]{3,2,1,0:T(8,128)S(1)}, u32[]{:S(2)}, u32[]{:S(2)}) async-start(f32[64,4,16,128]{3,2,1,0:T(8,128)} %pack.1), calls=%async_computation | async-start | bytes 4194304 | tf_op jit(solution)/shard_map/all_to_all | solution.py:494
  89.0 30.5 %all-to-all-done = f32[64,4,16,128]{3,2,1,0:T(8,128)S(1)} async-done(((f32[64,4,16,128]{3,2,1,0:T(8,128)}), f32[64,4,16,128]{3,2,1,0:T(8,128)S(1)}, u32[]{:S(2)}, u32[]{:S(2)}) %all-to-all-start) | async-done | bytes 2097184 | tf_op jit(solution)/shard_map/all_to_all | solution.py:494
  119.6 2.5 %route.1 = f32[64,4,16,128]{3,2,1,0:T(8,128)S(1)} custom-call(s32[256]{0:T(256)S(1)} %reshape.12.source, s32[128]{0:T(128)S(1)} %reshape.13.fix, bf16[32,128]{1,0:T(8,128)(2,1)S(1)} %copy-done.20, bf16[2,128,512]{2,1,0:T(8,128)(2,1)S(1)} %copy-done.17, f32[1,2048]{1,0:T(1,128)S(1)} %broadcast_in_dim_reshape.3.flipped, f32[256,16,128]{2,1,0:T(8,128)S(1)} %bitcast.25), custom_call_target="tpu_custom_call" | custom-call | flops 268435456 | bytes 4194304 | tf_op jit(solution)/shard_map/route/pallas_call | solution.py:324
  123.4 7.3 %all-to-all-start.1 = ((f32[64,4,16,128]{3,2,1,0:T(8,128)}), f32[64,4,16,128]{3,2,1,0:T(8,128)}, u32[]{:S(2)}, u32[]{:S(2)}) async-start(f32[64,4,16,128]{3,2,1,0:T(8,128)} %copy-done.4), calls=%async_computation.1 | async-start | bytes 4194304 | tf_op jit(solution)/shard_map/all_to_all | solution.py:494
  133.1 12.7 %collective-permute-start.8 = (f32[4,15,48,128]{3,2,1,0:T(8,128)S(1)}, f32[4,15,48,128]{3,2,1,0:T(8,128)S(1)}, u32[]{:S(2)}, u32[]{:S(2)}) collective-permute-start(f32[4,15,48,128]{3,2,1,0:T(8,128)S(1)} %get-tuple-element.32), channel_id=1, source_target_pairs={{0,1},{1,2},{2,3},{4,5},{5,6},{6,7},{8,9},{9,10},{10,11},{12,13},{... | collective-permute-start | bytes 4423688 | tf_op jit(solution)/shard_map/ppermute | solution.py:478
  145.8 2.1 collective-permute-start.9
  148.1 42.2 %collective-permute-done.8.below = f32[4,15,48,128]{3,2,1,0:T(8,128)S(1)} collective-permute-done((f32[4,15,48,128]{3,2,1,0:T(8,128)S(1)}, f32[4,15,48,128]{3,2,1,0:T(8,128)S(1)}, u32[]{:S(2)}, u32[]{:S(2)}) %collective-permute-start.8) | collective-permute-done | bytes 1474592 | tf_op jit(solution)/shard_map/ppermute | solution.py:478
  190.3 11.0 %collective-permute-done.9.above = f32[4,15,48,128]{3,2,1,0:T(8,128)S(1)} collective-permute-done((f32[4,15,48,128]{3,2,1,0:T(8,128)S(1)}, f32[4,15,48,128]{3,2,1,0:T(8,128)S(1)}, u32[]{:S(2)}, u32[]{:S(2)}) %collective-permute-start.9) | collective-permute-done | bytes 1474592 | tf_op jit(solution)/shard_map/ppermute | solution.py:478
  201.3 3.2 %radial.9.core = f32[4,16,48,128]{3,2,1,0:T(8,128)S(1)} custom-call(f32[4,15,48,128]{3,2,1,0:T(8,128)S(1)} %collective-permute-done.8.below, f32[4,16,48,128]{3,2,1,0:T(8,128)S(1)} %get-tuple-element.33.own, f32[4,15,48,128]{3,2,1,0:T(8,128)S(1)} %collective-permute-done.9.above), custom_call_target="tpu_custom_call" | custom-call | flops 36175872 | bytes 6094848 | tf_op jit(solution)/shard_map/radial/pallas_call | solution.py:218
  204.7 6.7 %base.1 = f32[4,16,128,128]{3,2,1,0:T(8,128)S(1)} custom-call(s32[4]{0:T(128)S(1)} %dynamic-slice_reduce_fusion.glued, bf16[256,256]{1,0:T(8,128)(2,1)S(1)} %copy-done.18, f32[128,160]{1,0:T(8,128)S(1)} %copy-done.22, f32[4,16,48,128]{3,2,1,0:T(8,128)S(1)} %radial.9.core, f32[16,80,128]{2,1,0:T(8,128)S(1)} %bitcast.33, f32[16,80,128]{2,1,0:T(8,128)S(1)} %bitcast.31, ...), custom_call_target="tpu_custom_call" | custom-call | flops 4294967296 | bytes 9437184 | tf_op jit(solution)/shard_map/base/pallas_call | solution.py:375
  213.4 2.2 copy-done.26
  215.6 12.2 %finish.1 = f32[3,16,128,128]{3,2,1,0:T(8,128)} custom-call(s32[4]{0:T(128)S(1)} %dynamic-slice_reduce_fusion.1.turned, bf16[2,128,128]{2,1,0:T(8,128)(2,1)S(1)} %copy-done.23, bf16[128,96]{1,0:T(8,128)(2,1)S(1)} %copy-done.24, bf16[384,512]{1,0:T(8,128)(2,1)S(1)} %copy-done.21, f32[64,4,16,128]{3,2,1,0:T(8,128)} %all-to-all-done.1.margins, ...), custom_call_target="tpu_custom_call" | custom-call | flops 4294967296 | bytes 9437184 | tf_op jit(solution)/shard_map/finish/pallas_call | solution.py:453
  (87 shorter events, 26.3 us)
Async XLA Ops:
  3.4 26.5 %collective-permute-start.5 = (f32[15,80,128]{2,1,0:T(8,128)S(1)}, f32[15,80,128]{2,1,0:T(8,128)S(1)}, u32[]{:S(2)}, u32[]{:S(2)}) collective-permute-start(f32[15,80,128]{2,1,0:T(8,128)S(1)} %get-tuple-element.28), channel_id=1, source_target_pairs={{1,0},{2,1},{3,2},{5,4},{6,5},{7,6},{9,8},{10,9},{11,10},{13,12},{... | collective-permute-start | bytes 1843208 | tf_op jit(solution)/shard_map/ppermute | solution.py:478
  8.5 26.3 %collective-permute-start.4 = (f32[15,80,128]{2,1,0:T(8,128)S(1)}, f32[15,80,128]{2,1,0:T(8,128)S(1)}, u32[]{:S(2)}, u32[]{:S(2)}) collective-permute-start(f32[15,80,128]{2,1,0:T(8,128)S(1)} %get-tuple-element.26), channel_id=1, source_target_pairs={{0,1},{1,2},{2,3},{4,5},{5,6},{6,7},{8,9},{9,10},{10,11},{12,13},{... | collective-permute-start | bytes 1843208 | tf_op jit(solution)/shard_map/ppermute | solution.py:478
  16.6 27.5 %collective-permute-start.6 = (f32[15,80,128]{2,1,0:T(8,128)S(1)}, f32[15,80,128]{2,1,0:T(8,128)S(1)}, u32[]{:S(2)}, u32[]{:S(2)}) collective-permute-start(f32[15,80,128]{2,1,0:T(8,128)S(1)} %get-tuple-element.29), channel_id=1, source_target_pairs={{0,1},{1,2},{2,3},{4,5},{5,6},{6,7},{8,9},{9,10},{10,11},{12,13},{... | collective-permute-start | bytes 1843208 | tf_op jit(solution)/shard_map/ppermute | solution.py:478
  19.1 27.8 %copy-start.27 = (s32[64,4]{0,1:T(4,128)S(1)}, s32[64,4]{0,1:T(4,128)}, u32[]{:S(2)}) copy-start(s32[64,4]{0,1:T(4,128)} %param.16) | copy-start | bytes 3076
  19.1 30.3 %collective-permute-start.7 = (f32[15,80,128]{2,1,0:T(8,128)}, f32[15,80,128]{2,1,0:T(8,128)}, u32[]{:S(2)}, u32[]{:S(2)}) collective-permute-start(f32[15,80,128]{2,1,0:T(8,128)} %get-tuple-element.31), channel_id=1, source_target_pairs={{1,0},{2,1},{3,2},{5,4},{6,5},{7,6},{9,8},{10,9},{11,10},{13,12},{... | collective-permute-start | bytes 1843208 | tf_op jit(solution)/shard_map/ppermute | solution.py:478
  22.3 29.5 %collective-permute-start.2 = (f32[15,80,128]{2,1,0:T(8,128)}, f32[15,80,128]{2,1,0:T(8,128)}, u32[]{:S(2)}, u32[]{:S(2)}) collective-permute-start(f32[15,80,128]{2,1,0:T(8,128)} %get-tuple-element.23), channel_id=1, source_target_pairs={{0,1},{1,2},{2,3},{4,5},{5,6},{6,7},{8,9},{9,10},{10,11},{12,13},{... | collective-permute-start | bytes 1843208 | tf_op jit(solution)/shard_map/ppermute | solution.py:478
  29.9 25.3 %collective-permute-start.3 = (f32[15,80,128]{2,1,0:T(8,128)}, f32[15,80,128]{2,1,0:T(8,128)}, u32[]{:S(2)}, u32[]{:S(2)}) collective-permute-start(f32[15,80,128]{2,1,0:T(8,128)} %get-tuple-element.25), channel_id=1, source_target_pairs={{1,0},{2,1},{3,2},{5,4},{6,5},{7,6},{9,8},{10,9},{11,10},{13,12},{... | collective-permute-start | bytes 1843208 | tf_op jit(solution)/shard_map/ppermute | solution.py:478
  35.6 24.5 %collective-permute-start = (f32[15,80,128]{2,1,0:T(8,128)}, f32[15,80,128]{2,1,0:T(8,128)}, u32[]{:S(2)}, u32[]{:S(2)}) collective-permute-start(f32[15,80,128]{2,1,0:T(8,128)} %get-tuple-element.20), channel_id=1, source_target_pairs={{0,1},{1,2},{2,3},{4,5},{5,6},{6,7},{8,9},{9,10},{10,11},{12,13},{... | collective-permute-start | bytes 1843208 | tf_op jit(solution)/shard_map/ppermute | solution.py:478
  44.9 18.1 %collective-permute-start.1 = (f32[15,80,128]{2,1,0:T(8,128)}, f32[15,80,128]{2,1,0:T(8,128)}, u32[]{:S(2)}, u32[]{:S(2)}) collective-permute-start(f32[15,80,128]{2,1,0:T(8,128)} %get-tuple-element.22), channel_id=1, source_target_pairs={{1,0},{2,1},{3,2},{5,4},{6,5},{7,6},{9,8},{10,9},{11,10},{13,12},{... | collective-permute-start | bytes 1843208 | tf_op jit(solution)/shard_map/ppermute | solution.py:478
  49.4 15.8 %copy-start.5 = (f32[1,16,80,128]{3,2,1,0:T(8,128)}, f32[1,16,80,128]{3,2,1,0:T(8,128)S(1)}, u32[]{:S(2)}) copy-start(f32[1,16,80,128]{3,2,1,0:T(8,128)S(1)} %radial.7) | copy-start | bytes 1966084
  51.8 13.4 %copy-start.7 = (f32[1,16,80,128]{3,2,1,0:T(8,128)}, f32[1,16,80,128]{3,2,1,0:T(8,128)S(1)}, u32[]{:S(2)}) copy-start(f32[1,16,80,128]{3,2,1,0:T(8,128)S(1)} %radial.8) | copy-start | bytes 1966084
  55.2 10.1 %copy-start.18 = (bf16[256,256]{1,0:T(8,128)(2,1)S(1)}, bf16[256,256]{1,0:T(8,128)(2,1)}, u32[]{:S(2)}) copy-start(bf16[256,256]{1,0:T(8,128)(2,1)} %constant.34.clone.pair) | copy-start | bytes 393220
  55.2 10.1 %copy-start.19 = (f32[4,16,128]{2,1,0:T(8,128)S(1)}, f32[4,16,128]{2,1,0:T(8,128)}, u32[]{:S(2)}) copy-start(f32[4,16,128]{2,1,0:T(8,128)} %constant.35.clone.picks) | copy-start | bytes 98308
  70.4 17.7 %copy-start.29 = (s32[64,4]{0,1:T(4,128)S(1)}, s32[64,4]{0,1:T(4,128)}, u32[]{:S(2)}) copy-start(s32[64,4]{0,1:T(4,128)} %param.17) | copy-start | bytes 3076
  70.4 18.2 %copy-start.28 = (s32[64,4]{0,1:T(4,128)S(1)}, s32[64,4]{0,1:T(4,128)}, u32[]{:S(2)}) copy-start(s32[64,4]{0,1:T(4,128)} %param.15) | copy-start | bytes 3076
  70.4 49.2 %copy-start.17 = (bf16[2,128,512]{2,1,0:T(8,128)(2,1)S(1)}, bf16[2,128,512]{2,1,0:T(8,128)(2,1)}, u32[]{:S(2)}) copy-start(bf16[2,128,512]{2,1,0:T(8,128)(2,1)} %constant.40.clone.corner) | copy-start | bytes 786436
  70.4 49.2 %copy-start.20 = (bf16[32,128]{1,0:T(8,128)(2,1)S(1)}, bf16[32,128]{1,0:T(8,128)(2,1)}, u32[]{:S(2)}) copy-start(bf16[32,128]{1,0:T(8,128)(2,1)} %constant.41.clone.ends) | copy-start | bytes 24580
  70.4 49.2 %all-to-all-start = ((f32[64,4,16,128]{3,2,1,0:T(8,128)}), f32[64,4,16,128]{3,2,1,0:T(8,128)S(1)}, u32[]{:S(2)}, u32[]{:S(2)}) async-start(f32[64,4,16,128]{3,2,1,0:T(8,128)} %pack.1), calls=%async_computation | async-start | bytes 4194304 | tf_op jit(solution)/shard_map/all_to_all | solution.py:494
  123.4 89.9 %all-to-all-start.1 = ((f32[64,4,16,128]{3,2,1,0:T(8,128)}), f32[64,4,16,128]{3,2,1,0:T(8,128)}, u32[]{:S(2)}, u32[]{:S(2)}) async-start(f32[64,4,16,128]{3,2,1,0:T(8,128)} %copy-done.4), calls=%async_computation.1 | async-start | bytes 4194304 | tf_op jit(solution)/shard_map/all_to_all | solution.py:494
  133.1 57.2 %collective-permute-start.8 = (f32[4,15,48,128]{3,2,1,0:T(8,128)S(1)}, f32[4,15,48,128]{3,2,1,0:T(8,128)S(1)}, u32[]{:S(2)}, u32[]{:S(2)}) collective-permute-start(f32[4,15,48,128]{3,2,1,0:T(8,128)S(1)} %get-tuple-element.32), channel_id=1, source_target_pairs={{0,1},{1,2},{2,3},{4,5},{5,6},{6,7},{8,9},{9,10},{10,11},{12,13},{... | collective-permute-start | bytes 4423688 | tf_op jit(solution)/shard_map/ppermute | solution.py:478
  145.8 55.5 %collective-permute-start.9 = (f32[4,15,48,128]{3,2,1,0:T(8,128)S(1)}, f32[4,15,48,128]{3,2,1,0:T(8,128)S(1)}, u32[]{:S(2)}, u32[]{:S(2)}) collective-permute-start(f32[4,15,48,128]{3,2,1,0:T(8,128)S(1)} %get-tuple-element.34), channel_id=1, source_target_pairs={{1,0},{2,1},{3,2},{5,4},{6,5},{7,6},{9,8},{10,9},{11,10},{13,12},{... | collective-permute-start | bytes 4423688 | tf_op jit(solution)/shard_map/ppermute | solution.py:478
  204.6 8.8 %copy-start.21 = (bf16[384,512]{1,0:T(8,128)(2,1)S(1)}, bf16[384,512]{1,0:T(8,128)(2,1)}, u32[]{:S(2)}) copy-start(bf16[384,512]{1,0:T(8,128)(2,1)} %constant.39.clone.spread) | copy-start | bytes 1179652
  204.6 8.7 %copy-start.23 = (bf16[2,128,128]{2,1,0:T(8,128)(2,1)S(1)}, bf16[2,128,128]{2,1,0:T(8,128)(2,1)}, u32[]{:S(2)}) copy-start(bf16[2,128,128]{2,1,0:T(8,128)(2,1)} %constant.37.clone.square) | copy-start | bytes 196612
  204.7 8.7 %copy-start.24 = (bf16[128,96]{1,0:T(8,128)(2,1)S(1)}, bf16[128,96]{1,0:T(8,128)(2,1)}, u32[]{:S(2)}) copy-start(bf16[128,96]{1,0:T(8,128)(2,1)} %constant.38.clone.ahead) | copy-start | bytes 73732
  (18 other events, 46.3 us)

commit v2 on v1

--- a/solution.py
+++ b/solution.py
@@ -54,7 +54,7 @@
     ahead_high, ahead_low = halves(np.concatenate([near.T, far.T], axis=1))
     eye = np.eye(4, dtype=np.float32)
     spread_high, spread_low = halves(np.concatenate([np.kron(eye, near), np.kron(eye, far)], axis=0))
-    corner = np.kron(eye, np.concatenate([near, far], axis=0))
+    corner_high, corner_low = halves(np.kron(eye, np.concatenate([near, far], axis=0)))
     ends = np.concatenate([pick_west, pick_east], axis=0)
     return dict(
         pair=pair,
@@ -63,7 +63,7 @@
         square=np.stack([high, low]),
         ahead=np.concatenate([ahead_high, ahead_high, ahead_low], axis=1),
         spread=np.concatenate([spread_high, spread_high, spread_low], axis=0),
-        corner=np.stack(halves(corner)),
+        corner=np.concatenate([corner_high, corner_high, corner_low], axis=0),
         ends=ends.astype(BF16),
     )
 
@@ -132,65 +132,53 @@
         down[l, at, :] = value
 
 
-def rim_kernel(weighted, *refs):
-    outs = refs[2 if weighted else 1 :]
+def levels_of(first, kernels, volume):
+    def rows(l, start, count):
+        w = volume[0, l, start : start + count, :]
+        product = w * kernels[0, l, start : start + count, :]
+        if first is None:
+            return product
+        field = jnp.full(w.shape, pl.program_id(0), jnp.int32)
+        return jnp.where(field == first, w, product)
+
+    return rows
+
+
+def rim_kernel(first, kernels, volume, own, up, down):
+    outs = own.at[0], up.at[0], down.at[0]
+    rows = levels_of(first, kernels, volume)
     for l in range(OWN):
-
-        def rows(start, count):
-            x = refs[0][0, l, start : start + count, :]
-            return x * refs[1][0, l, start : start + count, :] if weighted else x
-
-        levels_out(l, rows(0, DEEP), slice(0, DEEP), *outs)
-        levels_out(l, rows(SIDE - DEEP, DEEP), slice(DEEP, 2 * DEEP), *outs)
-        levels_out(l, rim_pairs(rows(DEEP, PAIRS), rows(UPPER, PAIRS)), slice(2 * DEEP, RIM), *outs)
-
-
-def rim_of(kernels, volume, field):
-    arrays = [volume] if field is None else [kernels, volume]
-    spec = [pl.BlockSpec((1, OWN, SIDE, SIDE), lambda i: (0, 0, 0, 0))]
-    if field is not None:
-        spec = [pl.BlockSpec((1, OWN, SIDE, SIDE), lambda i: (field, 0, 0, 0))] + spec
-    shapes = [jax.ShapeDtypeStruct((count, RIM, SIDE), F32) for count in (OWN, OWN - 1, OWN - 1)]
-    return pl.pallas_call(
-        functools.partial(rim_kernel, field is not None),
-        grid=(1,),
-        in_specs=spec,
-        out_specs=[pl.BlockSpec(x.shape, lambda i: (0, 0, 0)) for x in shapes],
-        out_shape=shapes,
-        name="rim",
-        compiler_params=ROOM,
-        cost_estimate=pl.CostEstimate(flops=1 << 20, bytes_accessed=4 << 20, transcendentals=0),
-    )(*arrays)
-
-
-def core_kernel(kernels, volume, own, up, down):
-    field = jnp.full((PAIRS, SIDE), pl.program_id(0), jnp.int32)
+        levels_out(l, rows(l, 0, DEEP), slice(0, DEEP), *outs)
+        levels_out(l, rows(l, SIDE - DEEP, DEEP), slice(DEEP, 2 * DEEP), *outs)
+        levels_out(l, rim_pairs(rows(l, DEEP, PAIRS), rows(l, UPPER, PAIRS)), slice(2 * DEEP, RIM), *outs)
+
+
+def core_kernel(first, kernels, volume, own, up, down):
+    outs = own.at[0], up.at[0], down.at[0]
+    rows = levels_of(first, kernels, volume)
     for l in range(OWN):
-        parts = []
-        for start in (DEEP, UPPER):
-            w = volume[l, start : start + PAIRS, :]
-            parts.append(jnp.where(field == 0, w, w * kernels[0, l, start : start + PAIRS, :]))
-        levels_out(l, core_pairs(*parts), slice(0, PAIRS), own.at[0], up.at[0], down.at[0])
-
-
-def core_of(kernels, volume):
+        levels_out(l, core_pairs(rows(l, DEEP, PAIRS), rows(l, UPPER, PAIRS)), slice(0, PAIRS), *outs)
+
+
+def part_of(kernel, rows, kernels, volume, fields):
+    start, count = fields[0], len(fields)
     counts = (OWN, OWN - 1, OWN - 1)
     return pl.pallas_call(
-        core_kernel,
-        grid=(4,),
+        functools.partial(kernel, 0 if start == 0 else None),
+        grid=(count,),
         in_specs=[
-            pl.BlockSpec((1, OWN, SIDE, SIDE), lambda i: (jnp.maximum(i - 1, 0), 0, 0, 0)),
-            pl.BlockSpec((OWN, SIDE, SIDE), lambda i: (0, 0, 0)),
+            pl.BlockSpec((1, OWN, SIDE, SIDE), lambda i: (jnp.maximum(i + start - 1, 0), 0, 0, 0)),
+            pl.BlockSpec((1, OWN, SIDE, SIDE), lambda i: (0, 0, 0, 0)),
         ],
-        out_specs=[pl.BlockSpec((1, c, PAIRS, SIDE), lambda i: (i, 0, 0, 0)) for c in counts],
-        out_shape=[jax.ShapeDtypeStruct((4, c, PAIRS, SIDE), F32) for c in counts],
-        name="core",
+        out_specs=[pl.BlockSpec((1, c, rows, SIDE), lambda i: (i, 0, 0, 0)) for c in counts],
+        out_shape=[jax.ShapeDtypeStruct((count, c, rows, SIDE), F32) for c in counts],
+        name="part",
         compiler_params=ROOM,
-        cost_estimate=pl.CostEstimate(flops=1 << 20, bytes_accessed=10 << 20, transcendentals=0),
+        cost_estimate=pl.CostEstimate(flops=1 << 20, bytes_accessed=count * 3 << 20, transcendentals=0),
     )(kernels, volume)
 
 
-def radial_kernel(below, own, above, out):
+def radial_rows(below, own, above, out):
     parts = (below, own, above)
 
     def tile(i, carry):
@@ -198,7 +186,7 @@
 
         def level(j):
             part, k = (0, j) if j < HALF else (1, j - HALF) if j < HALF + OWN else (2, j - HALF - OWN)
-            return parts[part][0, k, at, :]
+            return parts[part][k, at, :]
 
         x = [level(j) for j in range(SPAN)]
         for m in range(OWN):
@@ -206,10 +194,14 @@
             total = TAPS[0] * x[c]
             for k in range(1, HALF + 1):
                 total = total + TAPS[k] * (x[c - k] + x[c + k])
-            out[0, m, at, :] = total
+            out[m, at, :] = total
         return carry
 
-    lax.fori_loop(0, out.shape[2] // 8, tile, 0)
+    lax.fori_loop(0, out.shape[1] // 8, tile, 0)
+
+
+def radial_kernel(*refs):
+    radial_rows(*[r.at[0] for r in refs])
 
 
 def radial(below, own, above):
@@ -229,56 +221,68 @@
     )(below, own, above)
 
 
-def pack_kernel(field_count, glued, pair, picks, *refs):
-    fields = refs[:field_count]
-    out, edge, rows = refs[field_count:]
+def strips_kernel(glued, pair, picks, below, own, above, *refs):
+    out, rim, edge, rows = refs[-4:]
 
     def choose(side):
         raw = jnp.where(glued[side] < 2, 1.0, 0.0).astype(F32)
         return picks[side] * raw + picks[side + 2] * (1.0 - raw)
 
+    radial_rows(below.at[0], own.at[0], above.at[0], rim)
     left_high, left_low = split(jnp.concatenate([choose(0), choose(1)], axis=0))
     left = jnp.concatenate([left_high, left_low], axis=0)
-    for f in range(field_count):
-        rim = fields[f]
-        mine = pl.ds(f * OWN, OWN)
-        for q in range(OWN):
-            base = q * SIDE
-            rows[base : base + DEEP, :] = rim[q, :DEEP, :]
-            rows[base + SIDE - DEEP : base + SIDE, :] = rim[q, DEEP : 2 * DEEP, :]
-            first, second = unpair(rim[q, 2 * DEEP :, :], None)
-            rows[base + DEEP : base + UPPER, :] = first
-            rows[base + UPPER : base + SIDE - DEEP, :] = second
-        for d in range(DEEP):
-            edge[pl.ds(d, OWN, stride=DEEP), :] = rows[pl.ds(d, OWN, stride=SIDE), :]
-            edge[pl.ds(OWN * DEEP + d, OWN, stride=DEEP), :] = rows[pl.ds(SIDE - 1 - d, OWN, stride=SIDE), :]
-        raw = edge[...]
-        across = through(raw, pair[...])
-        for side in (2, 3):
-            at = slice((side - 2) * OWN * DEEP, (side - 1) * OWN * DEEP)
-            strip = jnp.where(glued[side] < 2, raw[at], across[at])
-            out[mine, side, :, :] = strip.reshape(OWN, DEEP, SIDE)
-        high, low = split(rows[...])
-        both = dot_t(left, high)
-        strips = both[: 2 * DEEP] + both[2 * DEEP :] + dot_t(left_high, low)
-        for q in range(OWN):
-            plane = strips[:, q * SIDE : (q + 1) * SIDE]
-            out[f * OWN + q, 0, :, :] = plane[:DEEP]
-            out[f * OWN + q, 1, :, :] = plane[DEEP:]
-
-
-def pack(rims, glued, const):
-    count = len(rims)
+    for q in range(OWN):
+        base = q * SIDE
+        rows[base : base + DEEP, :] = rim[q, :DEEP, :]
+        rows[base + SIDE - DEEP : base + SIDE, :] = rim[q, DEEP : 2 * DEEP, :]
+        first, second = unpair(rim[q, 2 * DEEP :, :], None)
+        rows[base + DEEP : base + UPPER, :] = first
+        rows[base + UPPER : base + SIDE - DEEP, :] = second
+    for d in range(DEEP):
+        edge[pl.ds(d, OWN, stride=DEEP), :] = rows[pl.ds(d, OWN, stride=SIDE), :]
+        edge[pl.ds(OWN * DEEP + d, OWN, stride=DEEP), :] = rows[pl.ds(SIDE - 1 - d, OWN, stride=SIDE), :]
+    raw = edge[...]
+    across = through(raw, pair[...])
+    for side in (2, 3):
+        at = slice((side - 2) * OWN * DEEP, (side - 1) * OWN * DEEP)
+        strip = jnp.where(glued[side] < 2, raw[at], across[at])
+        out[:, side, :, :] = strip.reshape(OWN, DEEP, SIDE)
+    high, low = split(rows[...])
+    both = dot_t(left, high)
+    strips = both[: 2 * DEEP] + both[2 * DEEP :] + dot_t(left_high, low)
+    for q in range(OWN):
+        plane = strips[:, q * SIDE : (q + 1) * SIDE]
+        out[q, 0, :, :] = plane[:DEEP]
+        out[q, 1, :, :] = plane[DEEP:]
+
+
+def add_strips(strips, field, halo, place, glued, const):
+    arrays = [glued, const["pair"], const["picks"], *halo]
+    specs = [SMEM] + [pl.BlockSpec(a.shape, lambda i, n=a.ndim: (0,) * n) for a in arrays[1:3]]
+    specs += [pl.BlockSpec((1,) + a.shape[1:], lambda i: (place, 0, 0, 0)) for a in halo]
+    aliases = {}
+    if strips is not None:
+        aliases = {len(arrays): 0}
+        arrays.append(strips)
+        specs.append(pl.BlockSpec(memory_space=pl.ANY))
     return pl.pallas_call(
-        functools.partial(pack_kernel, count),
-        in_specs=[SMEM] + [VMEM] * (2 + count),
-        out_specs=VMEM,
-        out_shape=jax.ShapeDtypeStruct((count * OWN, 4, DEEP, SIDE), F32),
+        strips_kernel,
+        grid=(1,),
+        in_specs=specs,
+        out_specs=[
+            pl.BlockSpec((OWN, 4, DEEP, SIDE), lambda i: (field, 0, 0, 0)),
+            pl.BlockSpec((OWN, RIM, SIDE), lambda i: (0, 0, 0)),
+        ],
+        out_shape=[
+            jax.ShapeDtypeStruct((4 * OWN, 4, DEEP, SIDE), F32),
+            jax.ShapeDtypeStruct((OWN, RIM, SIDE), F32),
+        ],
         scratch_shapes=[pltpu.VMEM((2 * OWN * DEEP, SIDE), F32), pltpu.VMEM((OWN * SIDE, SIDE), F32)],
-        name="pack",
+        input_output_aliases=aliases,
+        name="strips",
         compiler_params=ROOM,
-        cost_estimate=pl.CostEstimate(flops=1 << 29, bytes_accessed=6 << 20, transcendentals=0),
-    )(glued, const["pair"], const["picks"], *rims)
+        cost_estimate=pl.CostEstimate(flops=1 << 27, bytes_accessed=3 << 20, transcendentals=0),
+    )(*arrays)
 
 
 def route_kernel(source, fix, ends, corner, flipped, strips, out, patch):
@@ -287,35 +291,36 @@
 
     def move(i, carry):
         for j in range(8):
-            e = i * 8 + j
-            t, s = i * 2 + j // 4, j % 4
-            out[t, s, :, :] = strips[source[e], :, :]
+            t, s = i * 4 + j // 2, j % 2
+            out[t, s, :, :] = strips[source[t * 4 + s], :, :]
         return carry
 
-    lax.fori_loop(0, tiles // 2, move, 0)
+    lax.fori_loop(0, tiles // 4, move, 0)
     margins = out[:, 0:2, :, :].reshape(tiles * 2 * DEEP, SIDE)
     high, low = split(margins)
     seen = dot_t(ends[...], high) + dot_t(ends[...], low)
     first, last = seen[:DEEP], seen[DEEP:]
     swap = flipped[...] > 0.5
     turned = jnp.concatenate([jnp.where(swap, last, first), jnp.where(swap, first, last)], axis=0)
-    high, low = split(turned)
-    for g in range(tiles // group):
-        at = slice(g * SIDE, (g + 1) * SIDE)
-        added = dot(high[:, at], corner[0]) + dot(high[:, at], corner[1]) + dot(low[:, at], corner[0])
+    groups = tiles // group
+    high, low = [
+        jnp.concatenate([x[:, g * SIDE : (g + 1) * SIDE] for g in range(groups)], axis=0) for x in split(turned)
+    ]
+    added = dot(jnp.concatenate([high, low], axis=1), corner[: 2 * SIDE]) + dot(high, corner[2 * SIDE :])
+    for g in range(groups):
         for j in range(group):
-            block = added[:, j * SIDE : (j + 1) * SIDE]
+            block = added[g * 2 * DEEP : (g + 1) * 2 * DEEP, j * SIDE : (j + 1) * SIDE]
             patch[(g * group + j) * 2] = block[:DEEP]
             patch[(g * group + j) * 2 + 1] = block[DEEP:]
     patch[tiles * 2] = jnp.zeros((DEEP, SIDE), F32)
 
     def mend(i, carry):
-        for j in range(4):
-            t, s = i * 2 + j // 2, 2 + j % 2
-            out[t, s, :, :] = out[t, s, :, :] + patch[fix[i * 4 + j], :, :]
+        for j in range(8):
+            t, s = i * 4 + j // 2, j % 2
+            out[t, 2 + s, :, :] = strips[source[t * 4 + 2 + s], :, :] + patch[fix[t * 2 + s], :, :]
         return carry
 
-    lax.fori_loop(0, tiles // 2, mend, 0)
+    lax.fori_loop(0, tiles // 4, mend, 0)
 
 
 def route(strips, tables, const):
@@ -333,9 +338,9 @@
     )(source, fix, const["ends"], const["corner"], flipped, strips.reshape(tiles * 4, DEEP, SIDE))
 
 
-def base_kernel(glued, pair, along, core, *refs):
-    rims = refs[:4]
-    out, rows, across = refs[4:]
+def base_kernel(glued, pair, along, *refs):
+    cores, rims = refs[:2], refs[2:6]
+    out, rows, across = refs[6:]
     f = pl.program_id(0)
     lane = lanes((SIDE, along.shape[1]))
     south = jnp.where(glued[2] < 2, 1.0, 0.0).astype(F32)
@@ -351,7 +356,7 @@
                 base = q * SIDE
                 rows[base : base + DEEP, :] = rims[k][q, :DEEP, :]
                 rows[base + SIDE - DEEP : base + SIDE, :] = rims[k][q, DEEP : 2 * DEEP, :]
-                first, second = unpair(rims[k][q, 2 * DEEP :, :], core[0, q])
+                first, second = unpair(rims[k][q, 2 * DEEP :, :], cores[min(k, 1)][0, q])
                 rows[base + DEEP : base + UPPER, :] = first
                 rows[base + UPPER : base + SIDE - DEEP, :] = second
 
@@ -370,7 +375,7 @@
         out[0, q + 1] = total[:, SIDE:]
 
 
-def base_lateral(rims, core, glued, const):
+def base_lateral(rims, cores, glued, const):
     plane = (1, OWN, SIDE, SIDE)
     return pl.pallas_call(
         base_kernel,
@@ -379,7 +384,8 @@
             SMEM,
             pl.BlockSpec(const["pair"].shape, lambda i: (0, 0)),
             pl.BlockSpec(const["along"].shape, lambda i: (0, 0)),
-            pl.BlockSpec((1, OWN, PAIRS, SIDE), lambda i: (i, 0, 0, 0)),
+            pl.BlockSpec((1, OWN, PAIRS, SIDE), lambda i: (0, 0, 0, 0)),
+            pl.BlockSpec((1, OWN, PAIRS, SIDE), lambda i: (jnp.maximum(i - 1, 0), 0, 0, 0)),
         ]
         + [pl.BlockSpec((OWN, RIM, SIDE), lambda i: (0, 0, 0))] * 4,
         out_specs=pl.BlockSpec(plane, lambda i: (i, 0, 0, 0)),
@@ -388,7 +394,7 @@
         name="base",
         compiler_params=ROOM,
         cost_estimate=pl.CostEstimate(flops=1 << 32, bytes_accessed=9 << 20, transcendentals=0),
-    )(glued, const["pair"], const["along"], core, *rims)
+    )(glued, const["pair"], const["along"], *cores, *rims)
 
 
 def turn(code):
@@ -414,38 +420,51 @@
     def margin(side):
         return split(margins[:, side, :, :].reshape(size, SIDE))
 
-    sides = []
-    for side in (0, 1):
-        high, low = margin(side)
-        both = dot_t(ways[side].reshape(2 * SIDE, SIDE), high)
-        sides.append(both[:SIDE] + both[SIDE:] + dot_t(ways[side, 0], low))
-    rows = []
-    for side in (2, 3):
-        high, low = margin(side)
-        way = ways[side, 0]
-        rows.append((dot(high, way) + dot(low, way)).reshape(OWN, DEEP, SIDE))
-    planes = 4
-    for g in range(OWN // planes):
-        at = slice(g * planes * DEEP, (g + 1) * planes * DEEP)
-        high, low = split(jnp.concatenate([sides[0][:, at], sides[1][:, at]], axis=1))
-        left = jnp.concatenate([high, low], axis=1)
+    def planes_of(emit):
+        sides = []
+        for side in (0, 1):
+            high, low = margin(side)
+            both = dot_t(ways[side].reshape(2 * SIDE, SIDE), high)
+            sides.append(both[:SIDE] + both[SIDE:] + dot_t(ways[side, 0], low))
+        rows = []
+        for side in (2, 3):
+            high, low = margin(side)
+            way = ways[side, 0]
+            rows.append((dot(high, way) + dot(low, way)).reshape(OWN, DEEP, SIDE))
+        planes, groups = 4, 4
+        parts = []
+        for g in range(groups):
+            at = slice(g * planes * DEEP, (g + 1) * planes * DEEP)
+            parts.append(split(jnp.concatenate([sides[0][:, at], sides[1][:, at]], axis=1)))
+        high = jnp.concatenate([x for x, _ in parts], axis=0)
+        left = jnp.concatenate([high, jnp.concatenate([x for _, x in parts], axis=0)], axis=1)
         for j in range(0, planes, 2):
             to = slice(j * SIDE, (j + 2) * SIDE)
-            total = dot(left, spread[: 2 * SIDE, to]) + dot(high, spread[2 * SIDE :, to])
-            q = g * planes + j
-            pairs = [jnp.concatenate([rows[0][k], rows[1][k]], axis=0) for k in (q, q + 1)]
-            right, rest = split(jnp.concatenate(pairs, axis=1))
-            total = total + dot(ahead[...], jnp.concatenate([right, rest, right], axis=0))
-            for k in range(2):
-                plane = total[:, k * SIDE : (k + 1) * SIDE] + base[0, q + k]
-
-                @pl.when(f == 0)
-                def _():
-                    below[q + k] = 1.0 / plane
-
-                @pl.when(f > 0)
-                def _():
-                    out[0, q + k] = plane * below[q + k]
+            added = dot(left, spread[: 2 * SIDE, to])
+            for g in range(groups):
+                q = g * planes + j
+                pairs = [jnp.concatenate([rows[0][k], rows[1][k]], axis=0) for k in (q, q + 1)]
+                right, rest = split(jnp.concatenate(pairs, axis=1))
+                last = jnp.concatenate([parts[g][0], ahead[...]], axis=1)
+                total = added[g * SIDE : (g + 1) * SIDE] + dot(
+                    last, jnp.concatenate([spread[2 * SIDE :, to], right, rest, right], axis=0)
+                )
+                for k in range(2):
+                    emit(q + k, total[:, k * SIDE : (k + 1) * SIDE] + base[0, q + k])
+
+    @pl.when(f == 0)
+    def _():
+        def keep(q, plane):
+            below[q] = 1.0 / plane
+
+        planes_of(keep)
+
+    @pl.when(f > 0)
+    def _():
+        def divide(q, plane):
+            out[0, q] = plane * below[q]
+
+        planes_of(divide)
 
 
 def finish(base, margins, turned, const):
@@ -493,16 +512,25 @@
     def to_all(x):
         return lax.all_to_all(x, "tile", split_axis=0, concat_axis=0, tiled=True)
 
-    rims = []
-    for f in (None, 0, 1, 2):
-        parts = rim_of(kernels[0], volume, f)
-        rims.append(radial(*[x[None] for x in with_halo(*parts)])[0])
-    own, up, down = core_of(kernels[0], volume[0])
-    below, own, above = with_halo(own, up, down)
-    routed_in = to_all(pack(rims, glued, const))
+    def in_hbm(x):
+        return pltpu.with_memory_space_constraint(x, pltpu.HBM)
+
+    source_kernels, source_volume = in_hbm(kernels[0]), in_hbm(volume)
+    rims, strips = [], None
+    for fields in ((0,), (1, 2), (3,)):
+        parts = part_of(rim_kernel, RIM, source_kernels, source_volume, fields)
+        halo = with_halo(*parts)
+        for place, f in enumerate(fields):
+            strips, rim = add_strips(strips, f, halo, place, glued, const)
+            rims.append(in_hbm(rim))
+    cores = []
+    for fields in ((0,), (1, 2, 3)):
+        parts = part_of(core_kernel, PAIRS, source_kernels, source_volume, fields)
+        cores.append(with_halo(*parts))
+    routed_in = to_all(strips)
     routed = route(routed_in, tables, const)
     margins = to_all(routed)
-    base = base_lateral(rims, radial(below, own, above), glued, const)
+    base = in_hbm(base_lateral(rims, [radial(*x) for x in cores], glued, const))
     return finish(base, margins, turned, const)[None]
 
 

time: 229 us -> 245 us (1.070)
  waiting for transfers between devices: 94.3 us -> 102 us
  starting transfers between devices: 76.1 us -> 83.7 us
  Pallas kernels: 42.2 us -> 49.8 us
  local copies, waits for them, and re-layouts: 14.7 us -> 8.01 us
    pallas_call x6 -> x9, Pallas kernels: 9.36 us -> 29.1 us  [the longest x4 15.2 us: add_strips(): pl.pallas_call(strips_kernel, grid=(1,), in_specs=specs, out_specs=[pl.Bl...]
    ppermute x10, starting transfers between devices: 51.1 us -> 64.4 us  [with_halo(): return (lax.ppermute(up, 'slab', UP), own, lax.ppermute(down, 'slab', DOWN))]
    pallas_call x5 -> x2, Pallas kernels: 11.3 us -> 3.25 us  [radial(): pl.pallas_call(radial_kernel, grid=(count, rows // block), in_specs=[pl.B...]
    unnamed x60 -> x40, local copies, waits for them, and re-layouts: 13.4 us -> 6.79 us
    pallas_call x1, Pallas kernels: 12.2 us -> 6.29 us  [finish(): pl.pallas_call(finish_kernel, grid=(4,), in_specs=[SMEM, pl.BlockSpec(con...]
    all_to_all x2, starting transfers between devices: 25 us -> 19.3 us  [to_all(): return lax.all_to_all(x, 'tile', split_axis=0, concat_axis=0, tiled=True)]
    all_to_all x2, waiting for transfers between devices: 30.5 us -> 36.2 us  [to_all(): return lax.all_to_all(x, 'tile', split_axis=0, concat_axis=0, tiled=True)]
    ppermute x10, waiting for transfers between devices: 63.8 us -> 66.3 us  [with_halo(): return (lax.ppermute(up, 'slab', UP), own, lax.ppermute(down, 'slab', DOWN))]
  transfers between devices with their start and end apart: 12 -> 12, of which waited for: 7 -> 6; matrix products, arithmetic and copies ran while one was open for 1% -> 1% of each run, Pallas kernels for 9% -> 14%
where the time goes in v2:
time: 245 us; the launch traced here: 244 us
  waiting for transfers between devices  102 us (42%)
  starting transfers between devices  83.7 us (34%)
  Pallas kernels  49.8 us (20%)
  local copies, waits for them, and re-layouts  8.01 us (3%)
    ppermute x10, waiting for transfers between devices, with_halo(): return (lax.ppermute(up, 'slab', UP), own, lax.ppermute(down, 'slab', DOWN))  66.3 us
    ppermute x10, starting transfers between devices, with_halo(): return (lax.ppermute(up, 'slab', UP), own, lax.ppermute(down, 'slab', DOWN))  64.4 us
    all_to_all x2, waiting for transfers between devices, to_all(): return lax.all_to_all(x, 'tile', split_axis=0, concat_axis=0, tiled=True)  36.2 us
    all_to_all x2, starting transfers between devices, to_all(): return lax.all_to_all(x, 'tile', split_axis=0, concat_axis=0, tiled=True)  19.3 us
    pallas_call x4, Pallas kernels, add_strips(): pl.pallas_call(strips_kernel, grid=(1,), in_specs=specs, out_specs=[pl.Bl...  15.2 us
    pallas_call x5, Pallas kernels, part_of(): pl.pallas_call(functools.partial(kernel, 0 if start == 0 else None), grid...  13.9 us
    pallas_call x1, Pallas kernels, base_lateral(): pl.pallas_call(base_kernel, grid=(4,), in_specs=[SMEM, pl.BlockSpec(const...  7.96 us
    unnamed x40, local copies, waits for them, and re-layouts  6.79 us
  transfers between devices with their start and end apart: 12, of which 6 were waited for; matrix products, arithmetic and copies ran while one was open for 1% of the time, Pallas kernels for 14%

profile of v2, /device:TPU:1, one launch (start us, length us, event | category | flops | bytes accessed | tf_op | source)
XLA Modules:
  0.0 244.4 jit_solution(347708771888691731)
XLA Ops:
  0.0 3.2 %part.6 = (f32[2,16,80,128]{3,2,1,0:T(8,128)S(1)}, f32[2,15,80,128]{3,2,1,0:T(8,128)}, f32[2,15,80,128]{3,2,1,0:T(8,128)}) custom-call(f32[3,16,128,128]{3,2,1,0:T(8,128)} %bitcast.4, f32[1,16,128,128]{3,2,1,0:T(8,128)} %volume.9), custom_call_target="tpu_custom_call" | custom-call | flops 1048576 | bytes 6291456 | tf_op jit(solution)/shard_map/part/pallas_call | solution.py:166
  3.2 10.2 %collective-permute-start.2 = (f32[2,15,80,128]{3,2,1,0:T(8,128)}, f32[2,15,80,128]{3,2,1,0:T(8,128)S(1)}, u32[]{:S(2)}, u32[]{:S(2)}) collective-permute-start(f32[2,15,80,128]{3,2,1,0:T(8,128)} %get-tuple-element.31), channel_id=1, source_target_pairs={{0,1},{1,2},{2,3},{4,5},{5,6},{6,7},{8,9},{9,10},{10,11},{12,13},{... | collective-permute-start | bytes 3686408 | tf_op jit(solution)/shard_map/ppermute | solution.py:497
  15.4 2.6 %part.7 = (f32[1,16,80,128]{3,2,1,0:T(8,128)S(1)}, f32[1,15,80,128]{3,2,1,0:T(8,128)S(1)}, f32[1,15,80,128]{3,2,1,0:T(8,128)}) custom-call(f32[3,16,128,128]{3,2,1,0:T(8,128)} %bitcast.5, f32[1,16,128,128]{3,2,1,0:T(8,128)} %volume.9), custom_call_target="tpu_custom_call" | custom-call | flops 1048576 | bytes 3145728 | tf_op jit(solution)/shard_map/part/pallas_call | solution.py:166
  18.0 7.5 %collective-permute-start.4 = (f32[1,15,80,128]{3,2,1,0:T(8,128)S(1)}, f32[1,15,80,128]{3,2,1,0:T(8,128)S(1)}, u32[]{:S(2)}, u32[]{:S(2)}) collective-permute-start(f32[1,15,80,128]{3,2,1,0:T(8,128)S(1)} %get-tuple-element.34), channel_id=1, source_target_pairs={{0,1},{1,2},{2,3},{4,5},{5,6},{6,7},{8,9},{9,10},{10,11},{12,13},{... | collective-permute-start | bytes 1843208 | tf_op jit(solution)/shard_map/ppermute | solution.py:497
  27.6 2.9 %part.5 = (f32[1,16,80,128]{3,2,1,0:T(8,128)S(1)}, f32[1,15,80,128]{3,2,1,0:T(8,128)}, f32[1,15,80,128]{3,2,1,0:T(8,128)}) custom-call(f32[3,16,128,128]{3,2,1,0:T(8,128)} %bitcast.6, f32[1,16,128,128]{3,2,1,0:T(8,128)} %volume.9), custom_call_target="tpu_custom_call" | custom-call | flops 1048576 | bytes 3145728 | tf_op jit(solution)/shard_map/part/pallas_call | solution.py:166
  30.5 7.5 %collective-permute-start = (f32[1,15,80,128]{3,2,1,0:T(8,128)}, f32[1,15,80,128]{3,2,1,0:T(8,128)}, u32[]{:S(2)}, u32[]{:S(2)}) collective-permute-start(f32[1,15,80,128]{3,2,1,0:T(8,128)} %get-tuple-element.28), channel_id=1, source_target_pairs={{0,1},{1,2},{2,3},{4,5},{5,6},{6,7},{8,9},{9,10},{10,11},{12,13},{... | collective-permute-start | bytes 1843208 | tf_op jit(solution)/shard_map/ppermute | solution.py:497
  41.5 5.8 %collective-permute-done.5.above = f32[1,15,80,128]{3,2,1,0:T(8,128)} collective-permute-done((f32[1,15,80,128]{3,2,1,0:T(8,128)}, f32[1,15,80,128]{3,2,1,0:T(8,128)}, u32[]{:S(2)}, u32[]{:S(2)}) %collective-permute-start.5) | collective-permute-done | bytes 614432 | tf_op jit(solution)/shard_map/ppermute | solution.py:497
  49.4 3.6 %strips.4 = (f32[64,4,16,128]{3,2,1,0:T(8,128)}, f32[16,80,128]{2,1,0:T(8,128)S(1)}) custom-call(s32[4]{0:T(128)S(1)} %dynamic-slice_reduce_fusion.glued, bf16[256,256]{1,0:T(8,128)(2,1)S(1)} %copy-done, f32[4,16,128]{2,1,0:T(8,128)S(1)} %copy-done.5, f32[1,15,80,128]{3,2,1,0:T(8,128)S(1)} %copy-done.4, f32[1,16,80,128]{3,2,1,0:T(8,128)S(1)} %copy-done.2, ...), custom_call_target="tpu_custom_call" | custom-call | flops 134217728 | bytes 3145728 | tf_op jit(solution)/shard_map/strips/pallas_call | solution.py:268
  53.1 3.9 %strips.5 = (f32[64,4,16,128]{3,2,1,0:T(8,128)}, f32[16,80,128]{2,1,0:T(8,128)S(1)}) custom-call(s32[4]{0:T(128)S(1)} %dynamic-slice_reduce_fusion.glued, bf16[256,256]{1,0:T(8,128)(2,1)S(1)} %copy-done, f32[4,16,128]{2,1,0:T(8,128)S(1)} %copy-done.5, f32[2,15,80,128]{3,2,1,0:T(8,128)S(1)} %collective-permute-done.2.below, ...), custom_call_target="tpu_custom_call", output_to_operand_aliasing={{0}: (6, {})} | custom-call | flops 134217728 | bytes 3145728 | tf_op jit(solution)/shard_map/strips/pallas_call | solution.py:268
  56.9 3.9 %strips.6 = (f32[64,4,16,128]{3,2,1,0:T(8,128)}, f32[16,80,128]{2,1,0:T(8,128)S(1)}) custom-call(s32[4]{0:T(128)S(1)} %dynamic-slice_reduce_fusion.glued, bf16[256,256]{1,0:T(8,128)(2,1)S(1)} %copy-done, f32[4,16,128]{2,1,0:T(8,128)S(1)} %copy-done.5, f32[2,15,80,128]{3,2,1,0:T(8,128)S(1)} %collective-permute-done.2.below, ...), custom_call_target="tpu_custom_call", output_to_operand_aliasing={{0}: (6, {})} | custom-call | flops 134217728 | bytes 3145728 | tf_op jit(solution)/shard_map/strips/pallas_call | solution.py:268
  61.7 13.5 %collective-permute-done.1.above = f32[1,15,80,128]{3,2,1,0:T(8,128)} collective-permute-done((f32[1,15,80,128]{3,2,1,0:T(8,128)}, f32[1,15,80,128]{3,2,1,0:T(8,128)}, u32[]{:S(2)}, u32[]{:S(2)}) %collective-permute-start.1) | collective-permute-done | bytes 614432 | tf_op jit(solution)/shard_map/ppermute | solution.py:497
  75.2 3.8 %strips.7 = (f32[64,4,16,128]{3,2,1,0:T(8,128)}, f32[16,80,128]{2,1,0:T(8,128)S(1)}) custom-call(s32[4]{0:T(128)S(1)} %dynamic-slice_reduce_fusion.glued, bf16[256,256]{1,0:T(8,128)(2,1)S(1)} %copy-done, f32[4,16,128]{2,1,0:T(8,128)S(1)} %copy-done.5, f32[1,15,80,128]{3,2,1,0:T(8,128)} %collective-permute-done.below, ...), custom_call_target="tpu_custom_call", output_to_operand_aliasing={{0}: (6, {})} | custom-call | flops 134217728 | bytes 3145728 | tf_op jit(solution)/shard_map/strips/pallas_call | solution.py:268
  79.9 14.6 %all-to-all-start = ((f32[64,4,16,128]{3,2,1,0:T(8,128)}), f32[64,4,16,128]{3,2,1,0:T(8,128)S(1)}, u32[]{:S(2)}, u32[]{:S(2)}) async-start(f32[64,4,16,128]{3,2,1,0:T(8,128)} %get-tuple-element.40), calls=%async_computation | async-start | bytes 4194304 | tf_op jit(solution)/shard_map/all_to_all | solution.py:513
  95.5 36.2 %all-to-all-done = f32[64,4,16,128]{3,2,1,0:T(8,128)S(1)} async-done(((f32[64,4,16,128]{3,2,1,0:T(8,128)}), f32[64,4,16,128]{3,2,1,0:T(8,128)S(1)}, u32[]{:S(2)}, u32[]{:S(2)}) %all-to-all-start) | async-done | bytes 2097184 | tf_op jit(solution)/shard_map/all_to_all | solution.py:513
  131.6 3.2 %route.1 = f32[64,4,16,128]{3,2,1,0:T(8,128)} custom-call(s32[256]{0:T(256)S(1)} %reshape.12.source, s32[128]{0:T(128)S(1)} %reshape.13.fix, bf16[32,128]{1,0:T(8,128)(2,1)S(1)} %copy-done.7, bf16[384,512]{1,0:T(8,128)(2,1)S(1)} %copy-done.6, f32[1,2048]{1,0:T(1,128)S(1)} %broadcast_in_dim_reshape.3.flipped, f32[256,16,128]{2,1,0:T(8,128)S(1)} %bitcast.3), custom_call_target="tpu_custom_call" | custom-call | flops 268435456 | bytes 4194304 | tf_op jit(solution)/shard_map/route/pallas_call | solution.py:329
  134.9 4.7 %all-to-all-start.1 = ((f32[64,4,16,128]{3,2,1,0:T(8,128)}), f32[64,4,16,128]{3,2,1,0:T(8,128)S(1)}, u32[]{:S(2)}, u32[]{:S(2)}) async-start(f32[64,4,16,128]{3,2,1,0:T(8,128)} %route.1), calls=%async_computation.1 | async-start | bytes 4194304 | tf_op jit(solution)/shard_map/all_to_all | solution.py:513
  139.6 3.4 %part.9 = (f32[3,16,48,128]{3,2,1,0:T(8,128)S(1)}, f32[3,15,48,128]{3,2,1,0:T(8,128)S(1)}, f32[3,15,48,128]{3,2,1,0:T(8,128)S(1)}) custom-call(f32[3,16,128,128]{3,2,1,0:T(8,128)} %bitcast.7, f32[1,16,128,128]{3,2,1,0:T(8,128)} %volume.9), custom_call_target="tpu_custom_call" | custom-call | flops 1048576 | bytes 9437184 | tf_op jit(solution)/shard_map/part/pallas_call | solution.py:166
  142.9 21.7 %collective-permute-start.8 = (f32[3,15,48,128]{3,2,1,0:T(8,128)S(1)}, f32[3,15,48,128]{3,2,1,0:T(8,128)S(1)}, u32[]{:S(2)}, u32[]{:S(2)}) collective-permute-start(f32[3,15,48,128]{3,2,1,0:T(8,128)S(1)} %get-tuple-element.44), channel_id=1, source_target_pairs={{0,1},{1,2},{2,3},{4,5},{5,6},{6,7},{8,9},{9,10},{10,11},{12,13},{... | collective-permute-start | bytes 3317768 | tf_op jit(solution)/shard_map/ppermute | solution.py:497
  168.4 7.5 %collective-permute-start.6 = (f32[1,15,48,128]{3,2,1,0:T(8,128)S(1)}, f32[1,15,48,128]{3,2,1,0:T(8,128)S(1)}, u32[]{:S(2)}, u32[]{:S(2)}) collective-permute-start(f32[1,15,48,128]{3,2,1,0:T(8,128)S(1)} %get-tuple-element.41), channel_id=1, source_target_pairs={{0,1},{1,2},{2,3},{4,5},{5,6},{6,7},{8,9},{9,10},{10,11},{12,13},{... | collective-permute-start | bytes 1105928 | tf_op jit(solution)/shard_map/ppermute | solution.py:497
  178.2 22.4 %collective-permute-done.6.refs_0_ = f32[1,15,48,128]{3,2,1,0:T(8,128)S(1)} collective-permute-done((f32[1,15,48,128]{3,2,1,0:T(8,128)S(1)}, f32[1,15,48,128]{3,2,1,0:T(8,128)S(1)}, u32[]{:S(2)}, u32[]{:S(2)}) %collective-permute-start.6) | collective-permute-done | bytes 368672 | tf_op jit(solution)/shard_map/ppermute | solution.py:497
  200.7 24.1 %collective-permute-done.7.refs_2_ = f32[1,15,48,128]{3,2,1,0:T(8,128)S(1)} collective-permute-done((f32[1,15,48,128]{3,2,1,0:T(8,128)S(1)}, f32[1,15,48,128]{3,2,1,0:T(8,128)S(1)}, u32[]{:S(2)}, u32[]{:S(2)}) %collective-permute-start.7) | collective-permute-done | bytes 368672 | tf_op jit(solution)/shard_map/ppermute | solution.py:497
  225.6 2.4 %radial.3.refs_1_ = f32[3,16,48,128]{3,2,1,0:T(8,128)S(1)} custom-call(f32[3,15,48,128]{3,2,1,0:T(8,128)S(1)} %collective-permute-done.8.refs_0_, f32[3,16,48,128]{3,2,1,0:T(8,128)S(1)} %get-tuple-element.45.refs_1_, f32[3,15,48,128]{3,2,1,0:T(8,128)S(1)} %collective-permute-done.9.refs_2_), custom_call_target="tpu_custom_call" | custom-call | flops 27131904 | bytes 4571136 | tf_op jit(solution)/shard_map/radial/pallas_call | solution.py:210
  228.1 8.0 %base.1 = f32[4,16,128,128]{3,2,1,0:T(8,128)S(1)} custom-call(s32[4]{0:T(128)S(1)} %dynamic-slice_reduce_fusion.glued, bf16[256,256]{1,0:T(8,128)(2,1)S(1)} %copy-done, f32[128,160]{1,0:T(8,128)S(1)} %copy-done.13, f32[1,16,48,128]{3,2,1,0:T(8,128)S(1)} %radial.2.refs_0_, f32[3,16,48,128]{3,2,1,0:T(8,128)S(1)} %radial.3.refs_1_, f32[16,80,128]{2,1,0:T(8,128)} %copy-done.8, ...), custom_call_target="tpu_custom_call" | custom-call | flops 4294967296 | bytes 9437184 | tf_op jit(solution)/shard_map/base/pallas_call | solution.py:380
  238.1 6.3 %finish.1 = f32[3,16,128,128]{3,2,1,0:T(8,128)} custom-call(s32[4]{0:T(128)S(1)} %dynamic-slice_reduce_fusion.1.turned, bf16[2,128,128]{2,1,0:T(8,128)(2,1)S(1)} %copy-done.14, bf16[128,96]{1,0:T(8,128)(2,1)S(1)} %copy-done.15, bf16[384,512]{1,0:T(8,128)(2,1)S(1)} %copy-done.12, f32[64,4,16,128]{3,2,1,0:T(8,128)S(1)} %all-to-all-done.1.margins, ...), custom_call_target="tpu_custom_call" | custom-call | flops 4294967296 | bytes 9437184 | tf_op jit(solution)/shard_map/finish/pallas_call | solution.py:472
  (67 shorter events, 21.0 us)
Async XLA Ops:
  3.2 49.8 %collective-permute-start.2 = (f32[2,15,80,128]{3,2,1,0:T(8,128)}, f32[2,15,80,128]{3,2,1,0:T(8,128)S(1)}, u32[]{:S(2)}, u32[]{:S(2)}) collective-permute-start(f32[2,15,80,128]{3,2,1,0:T(8,128)} %get-tuple-element.31), channel_id=1, source_target_pairs={{0,1},{1,2},{2,3},{4,5},{5,6},{6,7},{8,9},{9,10},{10,11},{12,13},{... | collective-permute-start | bytes 3686408 | tf_op jit(solution)/shard_map/ppermute | solution.py:497
  13.4 39.6 %collective-permute-start.3 = (f32[2,15,80,128]{3,2,1,0:T(8,128)}, f32[2,15,80,128]{3,2,1,0:T(8,128)}, u32[]{:S(2)}, u32[]{:S(2)}) collective-permute-start(f32[2,15,80,128]{3,2,1,0:T(8,128)} %get-tuple-element.33), channel_id=1, source_target_pairs={{1,0},{2,1},{3,2},{5,4},{6,5},{7,6},{9,8},{10,9},{11,10},{13,12},{... | collective-permute-start | bytes 3686408 | tf_op jit(solution)/shard_map/ppermute | solution.py:497
  18.0 12.5 %copy-start.1 = (f32[1,16,80,128]{3,2,1,0:T(8,128)}, f32[1,16,80,128]{3,2,1,0:T(8,128)S(1)}, u32[]{:S(2)}) copy-start(f32[1,16,80,128]{3,2,1,0:T(8,128)S(1)} %get-tuple-element.35.own) | copy-start | bytes 1966084
  18.0 20.5 %collective-permute-start.4 = (f32[1,15,80,128]{3,2,1,0:T(8,128)S(1)}, f32[1,15,80,128]{3,2,1,0:T(8,128)S(1)}, u32[]{:S(2)}, u32[]{:S(2)}) collective-permute-start(f32[1,15,80,128]{3,2,1,0:T(8,128)S(1)} %get-tuple-element.34), channel_id=1, source_target_pairs={{0,1},{1,2},{2,3},{4,5},{5,6},{6,7},{8,9},{9,10},{10,11},{12,13},{... | collective-permute-start | bytes 1843208 | tf_op jit(solution)/shard_map/ppermute | solution.py:497
  25.5 15.8 %copy-start.17 = (s32[64,4]{0,1:T(4,128)S(1)}, s32[64,4]{0,1:T(4,128)}, u32[]{:S(2)}) copy-start(s32[64,4]{0,1:T(4,128)} %param.16) | copy-start | bytes 3076
  25.5 21.7 %copy-start = (bf16[256,256]{1,0:T(8,128)(2,1)S(1)}, bf16[256,256]{1,0:T(8,128)(2,1)}, u32[]{:S(2)}) copy-start(bf16[256,256]{1,0:T(8,128)(2,1)} %constant.34.clone.pair) | copy-start | bytes 393220
  25.6 21.7 %copy-start.5 = (f32[4,16,128]{2,1,0:T(8,128)S(1)}, f32[4,16,128]{2,1,0:T(8,128)}, u32[]{:S(2)}) copy-start(f32[4,16,128]{2,1,0:T(8,128)} %constant.35.clone.picks) | copy-start | bytes 98308
  25.6 21.7 %collective-permute-start.5 = (f32[1,15,80,128]{3,2,1,0:T(8,128)}, f32[1,15,80,128]{3,2,1,0:T(8,128)}, u32[]{:S(2)}, u32[]{:S(2)}) collective-permute-start(f32[1,15,80,128]{3,2,1,0:T(8,128)} %get-tuple-element.36), channel_id=1, source_target_pairs={{1,0},{2,1},{3,2},{5,4},{6,5},{7,6},{9,8},{10,9},{11,10},{13,12},{... | collective-permute-start | bytes 1843208 | tf_op jit(solution)/shard_map/ppermute | solution.py:497
  30.5 31.2 %collective-permute-start = (f32[1,15,80,128]{3,2,1,0:T(8,128)}, f32[1,15,80,128]{3,2,1,0:T(8,128)}, u32[]{:S(2)}, u32[]{:S(2)}) collective-permute-start(f32[1,15,80,128]{3,2,1,0:T(8,128)} %get-tuple-element.28), channel_id=1, source_target_pairs={{0,1},{1,2},{2,3},{4,5},{5,6},{6,7},{8,9},{9,10},{10,11},{12,13},{... | collective-permute-start | bytes 1843208 | tf_op jit(solution)/shard_map/ppermute | solution.py:497
  39.4 35.9 %collective-permute-start.1 = (f32[1,15,80,128]{3,2,1,0:T(8,128)}, f32[1,15,80,128]{3,2,1,0:T(8,128)}, u32[]{:S(2)}, u32[]{:S(2)}) collective-permute-start(f32[1,15,80,128]{3,2,1,0:T(8,128)} %get-tuple-element.30), channel_id=1, source_target_pairs={{1,0},{2,1},{3,2},{5,4},{6,5},{7,6},{9,8},{10,9},{11,10},{13,12},{... | collective-permute-start | bytes 1843208 | tf_op jit(solution)/shard_map/ppermute | solution.py:497
  53.0 3.9 %copy-start.8 = (f32[16,80,128]{2,1,0:T(8,128)}, f32[16,80,128]{2,1,0:T(8,128)S(1)}, u32[]{:S(2)}) copy-start(f32[16,80,128]{2,1,0:T(8,128)S(1)} %get-tuple-element.47.refs_2_) | copy-start | bytes 1966084
  79.9 14.6 %copy-start.19 = (s32[64,4]{0,1:T(4,128)S(1)}, s32[64,4]{0,1:T(4,128)}, u32[]{:S(2)}) copy-start(s32[64,4]{0,1:T(4,128)} %param.17) | copy-start | bytes 3076
  79.9 15.1 %copy-start.18 = (s32[64,4]{0,1:T(4,128)S(1)}, s32[64,4]{0,1:T(4,128)}, u32[]{:S(2)}) copy-start(s32[64,4]{0,1:T(4,128)} %param.15) | copy-start | bytes 3076
  79.9 51.7 %copy-start.6 = (bf16[384,512]{1,0:T(8,128)(2,1)S(1)}, bf16[384,512]{1,0:T(8,128)(2,1)}, u32[]{:S(2)}) copy-start(bf16[384,512]{1,0:T(8,128)(2,1)} %constant.40.clone.corner) | copy-start | bytes 1179652
  79.9 51.7 %copy-start.7 = (bf16[32,128]{1,0:T(8,128)(2,1)S(1)}, bf16[32,128]{1,0:T(8,128)(2,1)}, u32[]{:S(2)}) copy-start(bf16[32,128]{1,0:T(8,128)(2,1)} %constant.41.clone.ends) | copy-start | bytes 24580
  79.9 51.7 %all-to-all-start = ((f32[64,4,16,128]{3,2,1,0:T(8,128)}), f32[64,4,16,128]{3,2,1,0:T(8,128)S(1)}, u32[]{:S(2)}, u32[]{:S(2)}) async-start(f32[64,4,16,128]{3,2,1,0:T(8,128)} %get-tuple-element.40), calls=%async_computation | async-start | bytes 4194304 | tf_op jit(solution)/shard_map/all_to_all | solution.py:513
  134.9 103.2 %all-to-all-start.1 = ((f32[64,4,16,128]{3,2,1,0:T(8,128)}), f32[64,4,16,128]{3,2,1,0:T(8,128)S(1)}, u32[]{:S(2)}, u32[]{:S(2)}) async-start(f32[64,4,16,128]{3,2,1,0:T(8,128)} %route.1), calls=%async_computation.1 | async-start | bytes 4194304 | tf_op jit(solution)/shard_map/all_to_all | solution.py:513
  142.9 82.7 %collective-permute-start.8 = (f32[3,15,48,128]{3,2,1,0:T(8,128)S(1)}, f32[3,15,48,128]{3,2,1,0:T(8,128)S(1)}, u32[]{:S(2)}, u32[]{:S(2)}) collective-permute-start(f32[3,15,48,128]{3,2,1,0:T(8,128)S(1)} %get-tuple-element.44), channel_id=1, source_target_pairs={{0,1},{1,2},{2,3},{4,5},{5,6},{6,7},{8,9},{9,10},{10,11},{12,13},{... | collective-permute-start | bytes 3317768 | tf_op jit(solution)/shard_map/ppermute | solution.py:497
  164.6 61.0 %collective-permute-start.9 = (f32[3,15,48,128]{3,2,1,0:T(8,128)S(1)}, f32[3,15,48,128]{3,2,1,0:T(8,128)S(1)}, u32[]{:S(2)}, u32[]{:S(2)}) collective-permute-start(f32[3,15,48,128]{3,2,1,0:T(8,128)S(1)} %get-tuple-element.46), channel_id=1, source_target_pairs={{1,0},{2,1},{3,2},{5,4},{6,5},{7,6},{9,8},{10,9},{11,10},{13,12},{... | collective-permute-start | bytes 3317768 | tf_op jit(solution)/shard_map/ppermute | solution.py:497
  168.4 32.3 %collective-permute-start.6 = (f32[1,15,48,128]{3,2,1,0:T(8,128)S(1)}, f32[1,15,48,128]{3,2,1,0:T(8,128)S(1)}, u32[]{:S(2)}, u32[]{:S(2)}) collective-permute-start(f32[1,15,48,128]{3,2,1,0:T(8,128)S(1)} %get-tuple-element.41), channel_id=1, source_target_pairs={{0,1},{1,2},{2,3},{4,5},{5,6},{6,7},{8,9},{9,10},{10,11},{12,13},{... | collective-permute-start | bytes 1105928 | tf_op jit(solution)/shard_map/ppermute | solution.py:497
  175.9 48.8 %collective-permute-start.7 = (f32[1,15,48,128]{3,2,1,0:T(8,128)S(1)}, f32[1,15,48,128]{3,2,1,0:T(8,128)S(1)}, u32[]{:S(2)}, u32[]{:S(2)}) collective-permute-start(f32[1,15,48,128]{3,2,1,0:T(8,128)S(1)} %get-tuple-element.43), channel_id=1, source_target_pairs={{1,0},{2,1},{3,2},{5,4},{6,5},{7,6},{9,8},{10,9},{11,10},{13,12},{... | collective-permute-start | bytes 1105928 | tf_op jit(solution)/shard_map/ppermute | solution.py:497
  228.1 10.0 %copy-start.12 = (bf16[384,512]{1,0:T(8,128)(2,1)S(1)}, bf16[384,512]{1,0:T(8,128)(2,1)}, u32[]{:S(2)}) copy-start(bf16[384,512]{1,0:T(8,128)(2,1)} %constant.39.clone.spread) | copy-start | bytes 1179652
  228.1 10.0 %copy-start.14 = (bf16[2,128,128]{2,1,0:T(8,128)(2,1)S(1)}, bf16[2,128,128]{2,1,0:T(8,128)(2,1)}, u32[]{:S(2)}) copy-start(bf16[2,128,128]{2,1,0:T(8,128)(2,1)} %constant.37.clone.square) | copy-start | bytes 196612
  228.1 10.0 %copy-start.15 = (bf16[128,96]{1,0:T(8,128)(2,1)S(1)}, bf16[128,96]{1,0:T(8,128)(2,1)}, u32[]{:S(2)}) copy-start(bf16[128,96]{1,0:T(8,128)(2,1)} %constant.38.clone.ahead) | copy-start | bytes 73732
  (8 other events, 13.1 us)

commit v3 on v2

--- a/solution.py
+++ b/solution.py
@@ -124,12 +124,13 @@
     return jnp.where(edge, rolled(rim, 3 * QUARTER), inside[0]), jnp.where(edge, rolled(rim, QUARTER), inside[1])
 
 
-def levels_out(l, value, at, own, up, down):
-    own[l, at, :] = value
-    if l > 0:
-        up[l - 1, at, :] = value
-    if l < OWN - 1:
-        down[l, at, :] = value
+def halo_out(odd, own, near, cross):
+    def level(j, carry):
+        near[j, :, :] = own[j + 1 - odd[0], :, :]
+        cross[j, :, :] = own[j + odd[0], :, :]
+        return carry
+
+    lax.fori_loop(0, OWN - 1, level, 0)
 
 
 def levels_of(first, kernels, volume):
@@ -144,29 +145,30 @@
     return rows
 
 
-def rim_kernel(first, kernels, volume, own, up, down):
-    outs = own.at[0], up.at[0], down.at[0]
+def rim_kernel(first, odd, kernels, volume, own, near, cross):
     rows = levels_of(first, kernels, volume)
     for l in range(OWN):
-        levels_out(l, rows(l, 0, DEEP), slice(0, DEEP), *outs)
-        levels_out(l, rows(l, SIDE - DEEP, DEEP), slice(DEEP, 2 * DEEP), *outs)
-        levels_out(l, rim_pairs(rows(l, DEEP, PAIRS), rows(l, UPPER, PAIRS)), slice(2 * DEEP, RIM), *outs)
-
-
-def core_kernel(first, kernels, volume, own, up, down):
-    outs = own.at[0], up.at[0], down.at[0]
+        own[0, l, :DEEP, :] = rows(l, 0, DEEP)
+        own[0, l, DEEP : 2 * DEEP, :] = rows(l, SIDE - DEEP, DEEP)
+        own[0, l, 2 * DEEP :, :] = rim_pairs(rows(l, DEEP, PAIRS), rows(l, UPPER, PAIRS))
+    halo_out(odd, own.at[0], near.at[0], cross.at[0])
+
+
+def core_kernel(first, odd, kernels, volume, own, near, cross):
     rows = levels_of(first, kernels, volume)
     for l in range(OWN):
-        levels_out(l, core_pairs(rows(l, DEEP, PAIRS), rows(l, UPPER, PAIRS)), slice(0, PAIRS), *outs)
-
-
-def part_of(kernel, rows, kernels, volume, fields):
+        own[0, l] = core_pairs(rows(l, DEEP, PAIRS), rows(l, UPPER, PAIRS))
+    halo_out(odd, own.at[0], near.at[0], cross.at[0])
+
+
+def part_of(kernel, rows, odd, kernels, volume, fields):
     start, count = fields[0], len(fields)
     counts = (OWN, OWN - 1, OWN - 1)
     return pl.pallas_call(
         functools.partial(kernel, 0 if start == 0 else None),
         grid=(count,),
         in_specs=[
+            SMEM,
             pl.BlockSpec((1, OWN, SIDE, SIDE), lambda i: (jnp.maximum(i + start - 1, 0), 0, 0, 0)),
             pl.BlockSpec((1, OWN, SIDE, SIDE), lambda i: (0, 0, 0, 0)),
         ],
@@ -175,7 +177,7 @@
         name="part",
         compiler_params=ROOM,
         cost_estimate=pl.CostEstimate(flops=1 << 20, bytes_accessed=count * 3 << 20, transcendentals=0),
-    )(kernels, volume)
+    )(odd, kernels, volume)
 
 
 def radial_rows(below, own, above, out):
@@ -200,17 +202,28 @@
     lax.fori_loop(0, out.shape[1] // 8, tile, 0)
 
 
-def radial_kernel(*refs):
-    radial_rows(*[r.at[0] for r in refs])
-
-
-def radial(below, own, above):
+def radial_either(odd, near, own, cross, out):
+    @pl.when(odd[0] == 0)
+    def _():
+        radial_rows(cross, own, near, out)
+
+    @pl.when(odd[0] == 1)
+    def _():
+        radial_rows(near, own, cross, out)
+
+
+def radial_kernel(odd, *refs):
+    radial_either(odd, *[r.at[0] for r in refs])
+
+
+def radial(odd, near, own, cross):
     count, _, rows, _ = own.shape
     block = rows // 2
     return pl.pallas_call(
         radial_kernel,
         grid=(count, rows // block),
-        in_specs=[pl.BlockSpec((1, a.shape[1], block, SIDE), lambda f, i: (f, 0, i, 0)) for a in (below, own, above)],
+        in_specs=[SMEM]
+        + [pl.BlockSpec((1, a.shape[1], block, SIDE), lambda f, i: (f, 0, i, 0)) for a in (near, own, cross)],
         out_specs=pl.BlockSpec((1, OWN, block, SIDE), lambda f, i: (f, 0, i, 0)),
         out_shape=jax.ShapeDtypeStruct(own.shape, F32),
         name="radial",
@@ -218,17 +231,17 @@
         cost_estimate=pl.CostEstimate(
             flops=count * OWN * SPAN * rows * SIDE * 2, bytes_accessed=count * 62 * rows * 512, transcendentals=0
         ),
-    )(below, own, above)
-
-
-def strips_kernel(glued, pair, picks, below, own, above, *refs):
+    )(odd, near, own, cross)
+
+
+def strips_kernel(glued, odd, pair, picks, near, own, cross, *refs):
     out, rim, edge, rows = refs[-4:]
 
     def choose(side):
         raw = jnp.where(glued[side] < 2, 1.0, 0.0).astype(F32)
         return picks[side] * raw + picks[side + 2] * (1.0 - raw)
 
-    radial_rows(below.at[0], own.at[0], above.at[0], rim)
+    radial_either(odd, near.at[0], own.at[0], cross.at[0], rim)
     left_high, left_low = split(jnp.concatenate([choose(0), choose(1)], axis=0))
     left = jnp.concatenate([left_high, left_low], axis=0)
     for q in range(OWN):
@@ -256,9 +269,9 @@
         out[q, 1, :, :] = plane[DEEP:]
 
 
-def add_strips(strips, field, halo, place, glued, const):
-    arrays = [glued, const["pair"], const["picks"], *halo]
-    specs = [SMEM] + [pl.BlockSpec(a.shape, lambda i, n=a.ndim: (0,) * n) for a in arrays[1:3]]
+def add_strips(strips, field, halo, place, glued, odd, const):
+    arrays = [glued, odd, const["pair"], const["picks"], *halo]
+    specs = [SMEM] * 2 + [pl.BlockSpec(a.shape, lambda i, n=a.ndim: (0,) * n) for a in arrays[2:4]]
     specs += [pl.BlockSpec((1,) + a.shape[1:], lambda i: (place, 0, 0, 0)) for a in halo]
     aliases = {}
     if strips is not None:
@@ -356,7 +369,7 @@
                 base = q * SIDE
                 rows[base : base + DEEP, :] = rims[k][q, :DEEP, :]
                 rows[base + SIDE - DEEP : base + SIDE, :] = rims[k][q, DEEP : 2 * DEEP, :]
-                first, second = unpair(rims[k][q, 2 * DEEP :, :], cores[min(k, 1)][0, q])
+                first, second = unpair(rims[k][q, 2 * DEEP :, :], cores[k // 2][0, q])
                 rows[base + DEEP : base + UPPER, :] = first
                 rows[base + UPPER : base + SIDE - DEEP, :] = second
 
@@ -384,8 +397,8 @@
             SMEM,
             pl.BlockSpec(const["pair"].shape, lambda i: (0, 0)),
             pl.BlockSpec(const["along"].shape, lambda i: (0, 0)),
-            pl.BlockSpec((1, OWN, PAIRS, SIDE), lambda i: (0, 0, 0, 0)),
-            pl.BlockSpec((1, OWN, PAIRS, SIDE), lambda i: (jnp.maximum(i - 1, 0), 0, 0, 0)),
+            pl.BlockSpec((1, OWN, PAIRS, SIDE), lambda i: (jnp.minimum(i, 1), 0, 0, 0)),
+            pl.BlockSpec((1, OWN, PAIRS, SIDE), lambda i: (jnp.maximum(i - 2, 0), 0, 0, 0)),
         ]
         + [pl.BlockSpec((OWN, RIM, SIDE), lambda i: (0, 0, 0))] * 4,
         out_specs=pl.BlockSpec(plane, lambda i: (i, 0, 0, 0)),
@@ -489,12 +502,13 @@
     )(turned, const["square"], const["ahead"], const["spread"], margins, base)
 
 
-UP = [(0, 1), (1, 2), (2, 3)]
-DOWN = [(1, 0), (2, 1), (3, 2)]
-
-
-def with_halo(own, up, down):
-    return lax.ppermute(up, "slab", UP), own, lax.ppermute(down, "slab", DOWN)
+NEAR = [(0, 1), (1, 0), (2, 3), (3, 2)]
+CROSS = [(1, 2), (2, 1)]
+
+
+def with_halo(own, near, cross):
+    cross = lax.ppermute(cross, "slab", CROSS)
+    return lax.ppermute(near, "slab", NEAR), own, cross
 
 
 def per_device(kernels, volume, neighbours, glued_sides, reversals):
@@ -502,6 +516,7 @@
     tile = lax.axis_index("tile")
     glued = glued_sides[tile]
     turned = reversals[tile]
+    odd = (lax.axis_index("slab") % 2)[None]
     tiles = neighbours.shape[0]
     source = (neighbours * 4 + glued_sides).reshape(-1)
     ahead = glued_sides[:, 2:]
@@ -517,20 +532,20 @@
 
     source_kernels, source_volume = in_hbm(kernels[0]), in_hbm(volume)
     rims, strips = [], None
-    for fields in ((0,), (1, 2), (3,)):
-        parts = part_of(rim_kernel, RIM, source_kernels, source_volume, fields)
+    for fields in ((0, 1), (2,), (3,)):
+        parts = part_of(rim_kernel, RIM, odd, source_kernels, source_volume, fields)
         halo = with_halo(*parts)
         for place, f in enumerate(fields):
-            strips, rim = add_strips(strips, f, halo, place, glued, const)
+            strips, rim = add_strips(strips, f, halo, place, glued, odd, const)
             rims.append(in_hbm(rim))
     cores = []
-    for fields in ((0,), (1, 2, 3)):
-        parts = part_of(core_kernel, PAIRS, source_kernels, source_volume, fields)
+    for fields in ((0, 1), (2, 3)):
+        parts = part_of(core_kernel, PAIRS, odd, source_kernels, source_volume, fields)
         cores.append(with_halo(*parts))
     routed_in = to_all(strips)
     routed = route(routed_in, tables, const)
     margins = to_all(routed)
-    base = in_hbm(base_lateral(rims, [radial(*x) for x in cores], glued, const))
+    base = in_hbm(base_lateral(rims, [radial(odd, *x) for x in cores], glued, const))
     return finish(base, margins, turned, const)[None]
 
 

time: 245 us -> 224 us (0.914)
  starting transfers between devices: 83.7 us -> 65.6 us
    ppermute x10, starting transfers between devices: 64.4 us -> 31.3 us  [the longest x5 27.9 us: with_halo(): cross = lax.ppermute(cross, 'slab', CROSS)]
    all_to_all x2, starting transfers between devices: 19.3 us -> 34.3 us  [to_all(): return lax.all_to_all(x, 'tile', split_axis=0, concat_axis=0, tiled=True)]
    ppermute x10, waiting for transfers between devices: 66.3 us -> 54.5 us  [the longest x5 54.5 us: with_halo(): cross = lax.ppermute(cross, 'slab', CROSS)]
    all_to_all x2, waiting for transfers between devices: 36.2 us -> 45.8 us  [to_all(): return lax.all_to_all(x, 'tile', split_axis=0, concat_axis=0, tiled=True)]
    unnamed x40 -> x36, local copies, waits for them, and re-layouts: 6.79 us -> 5.42 us
  transfers between devices with their start and end apart: 12 -> 12, of which waited for: 6 -> 6; matrix products, arithmetic and copies ran while one was open for 1% -> 1% of each run, Pallas kernels for 14% -> 15%
where the time goes in v3:
time: 224 us; the launch traced here: 223 us
  waiting for transfers between devices  100 us (45%)
  starting transfers between devices  65.6 us (29%)
  Pallas kernels  50.1 us (22%)
  local copies, waits for them, and re-layouts  6.64 us (3%)
    ppermute x5, waiting for transfers between devices, with_halo(): cross = lax.ppermute(cross, 'slab', CROSS)  54.5 us
    all_to_all x2, waiting for transfers between devices, to_all(): return lax.all_to_all(x, 'tile', split_axis=0, concat_axis=0, tiled=True)  45.8 us
    all_to_all x2, starting transfers between devices, to_all(): return lax.all_to_all(x, 'tile', split_axis=0, concat_axis=0, tiled=True)  34.3 us
    ppermute x5, starting transfers between devices, with_halo(): cross = lax.ppermute(cross, 'slab', CROSS)  27.9 us
    pallas_call x4, Pallas kernels, add_strips(): pl.pallas_call(strips_kernel, grid=(1,), in_specs=specs, out_specs=[pl.Bl...  15 us
    pallas_call x5, Pallas kernels, part_of(): pl.pallas_call(functools.partial(kernel, 0 if start == 0 else None), grid...  14.2 us
    pallas_call x1, Pallas kernels, base_lateral(): pl.pallas_call(base_kernel, grid=(4,), in_specs=[SMEM, pl.BlockSpec(const...  7.96 us
    pallas_call x1, Pallas kernels, finish(): pl.pallas_call(finish_kernel, grid=(4,), in_specs=[SMEM, pl.BlockSpec(con...  6.31 us
  transfers between devices with their start and end apart: 12, of which 6 were waited for; matrix products, arithmetic and copies ran while one was open for 1% of the time, Pallas kernels for 15%

profile of v3, /device:TPU:1, one launch (start us, length us, event | category | flops | bytes accessed | tf_op | source)
XLA Modules:
  0.0 222.9 jit_solution(1695204492481890294)
XLA Ops:
  0.0 3.3 %part.7 = (f32[2,16,80,128]{3,2,1,0:T(8,128)S(1)}, f32[2,15,80,128]{3,2,1,0:T(8,128)S(1)}, f32[2,15,80,128]{3,2,1,0:T(8,128)}) custom-call(s32[1]{0:T(128)} %bitcast.odd, f32[3,16,128,128]{3,2,1,0:T(8,128)} %bitcast.5, f32[1,16,128,128]{3,2,1,0:T(8,128)} %volume.9), custom_call_target="tpu_custom_call" | custom-call | flops 1048576 | bytes 6291456 | tf_op jit(solution)/shard_map/part/pallas_call | solution.py:167
  3.3 3.2 %collective-permute-start.4 = (f32[2,15,80,128]{3,2,1,0:T(8,128)S(1)}, f32[2,15,80,128]{3,2,1,0:T(8,128)S(1)}, u32[]{:S(2)}, u32[]{:S(2)}) collective-permute-start(f32[2,15,80,128]{3,2,1,0:T(8,128)S(1)} %get-tuple-element.34), channel_id=1, source_target_pairs={{0,1},{1,0},{2,3},{3,2},{4,5},{5,4},{6,7},{7,6},{8,9},{9,8},{10,11... | collective-permute-start | bytes 3686408 | tf_op jit(solution)/shard_map/ppermute | solution.py:511
  6.5 7.0 %collective-permute-start.5 = (f32[2,15,80,128]{3,2,1,0:T(8,128)}, f32[2,15,80,128]{3,2,1,0:T(8,128)}, u32[]{:S(2)}, u32[]{:S(2)}) collective-permute-start(f32[2,15,80,128]{3,2,1,0:T(8,128)} %get-tuple-element.36), channel_id=1, source_target_pairs={{1,2},{2,1},{5,6},{6,5},{9,10},{10,9},{13,14},{14,13},{17,18},{18,... | collective-permute-start | bytes 3686408 | tf_op jit(solution)/shard_map/ppermute | solution.py:510
  13.5 3.1 %part.6 = (f32[1,16,80,128]{3,2,1,0:T(8,128)S(1)}, f32[1,15,80,128]{3,2,1,0:T(8,128)}, f32[1,15,80,128]{3,2,1,0:T(8,128)}) custom-call(s32[1]{0:T(128)} %bitcast.odd, f32[3,16,128,128]{3,2,1,0:T(8,128)} %bitcast.6, f32[1,16,128,128]{3,2,1,0:T(8,128)} %volume.9), custom_call_target="tpu_custom_call" | custom-call | flops 1048576 | bytes 3145728 | tf_op jit(solution)/shard_map/part/pallas_call | solution.py:167
  16.6 2.6 %collective-permute-start.3 = (f32[1,15,80,128]{3,2,1,0:T(8,128)}, f32[1,15,80,128]{3,2,1,0:T(8,128)}, u32[]{:S(2)}, u32[]{:S(2)}) collective-permute-start(f32[1,15,80,128]{3,2,1,0:T(8,128)} %get-tuple-element.33), channel_id=1, source_target_pairs={{1,2},{2,1},{5,6},{6,5},{9,10},{10,9},{13,14},{14,13},{17,18},{18,... | collective-permute-start | bytes 1843208 | tf_op jit(solution)/shard_map/ppermute | solution.py:510
  19.2 3.1 %part.5 = (f32[1,16,80,128]{3,2,1,0:T(8,128)S(1)}, f32[1,15,80,128]{3,2,1,0:T(8,128)}, f32[1,15,80,128]{3,2,1,0:T(8,128)}) custom-call(s32[1]{0:T(128)} %bitcast.odd, f32[3,16,128,128]{3,2,1,0:T(8,128)} %bitcast.7, f32[1,16,128,128]{3,2,1,0:T(8,128)} %volume.9), custom_call_target="tpu_custom_call" | custom-call | flops 1048576 | bytes 3145728 | tf_op jit(solution)/shard_map/part/pallas_call | solution.py:167
  22.3 7.0 %collective-permute-start.1 = (f32[1,15,80,128]{3,2,1,0:T(8,128)}, f32[1,15,80,128]{3,2,1,0:T(8,128)}, u32[]{:S(2)}, u32[]{:S(2)}) collective-permute-start(f32[1,15,80,128]{3,2,1,0:T(8,128)} %get-tuple-element.30), channel_id=1, source_target_pairs={{1,2},{2,1},{5,6},{6,5},{9,10},{10,9},{13,14},{14,13},{17,18},{18,... | collective-permute-start | bytes 1843208 | tf_op jit(solution)/shard_map/ppermute | solution.py:510
  29.5 4.8 %collective-permute-done.5.cross = f32[2,15,80,128]{3,2,1,0:T(8,128)} collective-permute-done((f32[2,15,80,128]{3,2,1,0:T(8,128)}, f32[2,15,80,128]{3,2,1,0:T(8,128)}, u32[]{:S(2)}, u32[]{:S(2)}) %collective-permute-start.5) | collective-permute-done | bytes 1228832 | tf_op jit(solution)/shard_map/ppermute | solution.py:510
  34.3 3.6 %strips.4 = (f32[64,4,16,128]{3,2,1,0:T(8,128)}, f32[16,80,128]{2,1,0:T(8,128)S(1)}) custom-call(s32[4]{0:T(128)S(1)} %dynamic-slice_reduce_fusion.glued, s32[1]{0:T(128)} %bitcast.odd, bf16[256,256]{1,0:T(8,128)(2,1)S(1)} %copy-done, f32[4,16,128]{2,1,0:T(8,128)S(1)} %copy-done.3, f32[2,15,80,128]{3,2,1,0:T(8,128)S(1)} %collective-permute-done.4.near, ...), custom_call_target="tpu_custom_call" | custom-call | flops 134217728 | bytes 3145728 | tf_op jit(solution)/shard_map/strips/pallas_call | solution.py:281
  38.8 3.7 %strips.5 = (f32[64,4,16,128]{3,2,1,0:T(8,128)}, f32[16,80,128]{2,1,0:T(8,128)S(1)}) custom-call(s32[4]{0:T(128)S(1)} %dynamic-slice_reduce_fusion.glued, s32[1]{0:T(128)} %bitcast.odd, bf16[256,256]{1,0:T(8,128)(2,1)S(1)} %copy-done, f32[4,16,128]{2,1,0:T(8,128)S(1)} %copy-done.3, ...), custom_call_target="tpu_custom_call", output_to_operand_aliasing={{0}: (7, {})} | custom-call | flops 134217728 | bytes 3145728 | tf_op jit(solution)/shard_map/strips/pallas_call | solution.py:281
  44.9 3.8 %strips.6 = (f32[64,4,16,128]{3,2,1,0:T(8,128)}, f32[16,80,128]{2,1,0:T(8,128)S(1)}) custom-call(s32[4]{0:T(128)S(1)} %dynamic-slice_reduce_fusion.glued, s32[1]{0:T(128)} %bitcast.odd, bf16[256,256]{1,0:T(8,128)(2,1)S(1)} %copy-done, f32[4,16,128]{2,1,0:T(8,128)S(1)} %copy-done.3, ...), custom_call_target="tpu_custom_call", output_to_operand_aliasing={{0}: (7, {})} | custom-call | flops 134217728 | bytes 3145728 | tf_op jit(solution)/shard_map/strips/pallas_call | solution.py:281
  49.6 9.6 %collective-permute-done.1.cross = f32[1,15,80,128]{3,2,1,0:T(8,128)} collective-permute-done((f32[1,15,80,128]{3,2,1,0:T(8,128)}, f32[1,15,80,128]{3,2,1,0:T(8,128)}, u32[]{:S(2)}, u32[]{:S(2)}) %collective-permute-start.1) | collective-permute-done | bytes 614432 | tf_op jit(solution)/shard_map/ppermute | solution.py:510
  59.2 3.8 %strips.7 = (f32[64,4,16,128]{3,2,1,0:T(8,128)}, f32[16,80,128]{2,1,0:T(8,128)S(1)}) custom-call(s32[4]{0:T(128)S(1)} %dynamic-slice_reduce_fusion.glued, s32[1]{0:T(128)} %bitcast.odd, bf16[256,256]{1,0:T(8,128)(2,1)S(1)} %copy-done, f32[4,16,128]{2,1,0:T(8,128)S(1)} %copy-done.3, ...), custom_call_target="tpu_custom_call", output_to_operand_aliasing={{0}: (7, {})} | custom-call | flops 134217728 | bytes 3145728 | tf_op jit(solution)/shard_map/strips/pallas_call | solution.py:281
  63.9 28.6 %all-to-all-start = ((f32[64,4,16,128]{3,2,1,0:T(8,128)}), f32[64,4,16,128]{3,2,1,0:T(8,128)S(1)}, u32[]{:S(2)}, u32[]{:S(2)}) async-start(f32[64,4,16,128]{3,2,1,0:T(8,128)} %get-tuple-element.40), calls=%async_computation | async-start | bytes 4194304 | tf_op jit(solution)/shard_map/all_to_all | solution.py:528
  93.5 45.8 %all-to-all-done = f32[64,4,16,128]{3,2,1,0:T(8,128)S(1)} async-done(((f32[64,4,16,128]{3,2,1,0:T(8,128)}), f32[64,4,16,128]{3,2,1,0:T(8,128)S(1)}, u32[]{:S(2)}, u32[]{:S(2)}) %all-to-all-start) | async-done | bytes 2097184 | tf_op jit(solution)/shard_map/all_to_all | solution.py:528
  139.2 3.2 %route.1 = f32[64,4,16,128]{3,2,1,0:T(8,128)} custom-call(s32[256]{0:T(256)S(1)} %reshape.12.source, s32[128]{0:T(128)S(1)} %reshape.13.fix, bf16[32,128]{1,0:T(8,128)(2,1)S(1)} %copy-done.5, bf16[384,512]{1,0:T(8,128)(2,1)S(1)} %copy-done.4, f32[1,2048]{1,0:T(1,128)S(1)} %broadcast_in_dim_reshape.3.flipped, f32[256,16,128]{2,1,0:T(8,128)S(1)} %bitcast.4), custom_call_target="tpu_custom_call" | custom-call | flops 268435456 | bytes 4194304 | tf_op jit(solution)/shard_map/route/pallas_call | solution.py:342
  142.5 5.7 %all-to-all-start.1 = ((f32[64,4,16,128]{3,2,1,0:T(8,128)}), f32[64,4,16,128]{3,2,1,0:T(8,128)S(1)}, u32[]{:S(2)}, u32[]{:S(2)}) async-start(f32[64,4,16,128]{3,2,1,0:T(8,128)} %route.1), calls=%async_computation.1 | async-start | bytes 4194304 | tf_op jit(solution)/shard_map/all_to_all | solution.py:528
  148.2 2.4 %part.8 = (f32[2,16,48,128]{3,2,1,0:T(8,128)S(1)}, f32[2,15,48,128]{3,2,1,0:T(8,128)S(1)}, f32[2,15,48,128]{3,2,1,0:T(8,128)S(1)}) custom-call(s32[1]{0:T(128)} %bitcast.odd, f32[3,16,128,128]{3,2,1,0:T(8,128)} %bitcast.8, f32[1,16,128,128]{3,2,1,0:T(8,128)} %volume.9), custom_call_target="tpu_custom_call" | custom-call | flops 1048576 | bytes 6291456 | tf_op jit(solution)/shard_map/part/pallas_call | solution.py:167
  150.7 9.2 %collective-permute-start.7 = (f32[2,15,48,128]{3,2,1,0:T(8,128)S(1)}, f32[2,15,48,128]{3,2,1,0:T(8,128)S(1)}, u32[]{:S(2)}, u32[]{:S(2)}) collective-permute-start(f32[2,15,48,128]{3,2,1,0:T(8,128)S(1)} %get-tuple-element.43), channel_id=1, source_target_pairs={{1,2},{2,1},{5,6},{6,5},{9,10},{10,9},{13,14},{14,13},{17,18},{18,... | collective-permute-start | bytes 2211848 | tf_op jit(solution)/shard_map/ppermute | solution.py:510
  159.9 2.4 %part.9 = (f32[2,16,48,128]{3,2,1,0:T(8,128)S(1)}, f32[2,15,48,128]{3,2,1,0:T(8,128)S(1)}, f32[2,15,48,128]{3,2,1,0:T(8,128)S(1)}) custom-call(s32[1]{0:T(128)} %bitcast.odd, f32[3,16,128,128]{3,2,1,0:T(8,128)} %bitcast.9, f32[1,16,128,128]{3,2,1,0:T(8,128)} %volume.9), custom_call_target="tpu_custom_call" | custom-call | flops 1048576 | bytes 6291456 | tf_op jit(solution)/shard_map/part/pallas_call | solution.py:167
  164.7 32.3 %collective-permute-done.7.refs_2_ = f32[2,15,48,128]{3,2,1,0:T(8,128)S(1)} collective-permute-done((f32[2,15,48,128]{3,2,1,0:T(8,128)S(1)}, f32[2,15,48,128]{3,2,1,0:T(8,128)S(1)}, u32[]{:S(2)}, u32[]{:S(2)}) %collective-permute-start.7) | collective-permute-done | bytes 737312 | tf_op jit(solution)/shard_map/ppermute | solution.py:510
  198.7 6.2 %collective-permute-done.9.refs_2_ = f32[2,15,48,128]{3,2,1,0:T(8,128)S(1)} collective-permute-done((f32[2,15,48,128]{3,2,1,0:T(8,128)S(1)}, f32[2,15,48,128]{3,2,1,0:T(8,128)S(1)}, u32[]{:S(2)}, u32[]{:S(2)}) %collective-permute-start.9) | collective-permute-done | bytes 737312 | tf_op jit(solution)/shard_map/ppermute | solution.py:510
  206.7 8.0 %base.1 = f32[4,16,128,128]{3,2,1,0:T(8,128)S(1)} custom-call(s32[4]{0:T(128)S(1)} %dynamic-slice_reduce_fusion.glued, bf16[256,256]{1,0:T(8,128)(2,1)S(1)} %copy-done, f32[128,160]{1,0:T(8,128)S(1)} %copy-done.11, f32[2,16,48,128]{3,2,1,0:T(8,128)S(1)} %radial.2.refs_0_, f32[2,16,48,128]{3,2,1,0:T(8,128)S(1)} %radial.3.refs_1_, f32[16,80,128]{2,1,0:T(8,128)} %copy-done.6, ...), custom_call_target="tpu_custom_call" | custom-call | flops 4294967296 | bytes 9437184 | tf_op jit(solution)/shard_map/base/pallas_call | solution.py:393
  216.6 6.3 %finish.1 = f32[3,16,128,128]{3,2,1,0:T(8,128)} custom-call(s32[4]{0:T(128)S(1)} %dynamic-slice_reduce_fusion.1.turned, bf16[2,128,128]{2,1,0:T(8,128)(2,1)S(1)} %copy-done.12, bf16[128,96]{1,0:T(8,128)(2,1)S(1)} %copy-done.13, bf16[384,512]{1,0:T(8,128)(2,1)S(1)} %copy-done.10, f32[64,4,16,128]{3,2,1,0:T(8,128)S(1)} %all-to-all-done.1.margins, ...), custom_call_target="tpu_custom_call" | custom-call | flops 4294967296 | bytes 9437184 | tf_op jit(solution)/shard_map/finish/pallas_call | solution.py:485
  (63 shorter events, 13.9 us)
Async XLA Ops:
  3.3 19.0 %collective-permute-start.4 = (f32[2,15,80,128]{3,2,1,0:T(8,128)S(1)}, f32[2,15,80,128]{3,2,1,0:T(8,128)S(1)}, u32[]{:S(2)}, u32[]{:S(2)}) collective-permute-start(f32[2,15,80,128]{3,2,1,0:T(8,128)S(1)} %get-tuple-element.34), channel_id=1, source_target_pairs={{0,1},{1,0},{2,3},{3,2},{4,5},{5,4},{6,7},{7,6},{8,9},{9,8},{10,11... | collective-permute-start | bytes 3686408 | tf_op jit(solution)/shard_map/ppermute | solution.py:511
  6.5 27.8 %collective-permute-start.5 = (f32[2,15,80,128]{3,2,1,0:T(8,128)}, f32[2,15,80,128]{3,2,1,0:T(8,128)}, u32[]{:S(2)}, u32[]{:S(2)}) collective-permute-start(f32[2,15,80,128]{3,2,1,0:T(8,128)} %get-tuple-element.36), channel_id=1, source_target_pairs={{1,2},{2,1},{5,6},{6,5},{9,10},{10,9},{13,14},{14,13},{17,18},{18,... | collective-permute-start | bytes 3686408 | tf_op jit(solution)/shard_map/ppermute | solution.py:510
  16.6 26.8 %collective-permute-start.2 = (f32[1,15,80,128]{3,2,1,0:T(8,128)}, f32[1,15,80,128]{3,2,1,0:T(8,128)}, u32[]{:S(2)}, u32[]{:S(2)}) collective-permute-start(f32[1,15,80,128]{3,2,1,0:T(8,128)} %get-tuple-element.31), channel_id=1, source_target_pairs={{0,1},{1,0},{2,3},{3,2},{4,5},{5,4},{6,7},{7,6},{8,9},{9,8},{10,11... | collective-permute-start | bytes 1843208 | tf_op jit(solution)/shard_map/ppermute | solution.py:511
  16.6 12.7 %copy-start.15 = (s32[64,4]{0,1:T(4,128)S(1)}, s32[64,4]{0,1:T(4,128)}, u32[]{:S(2)}) copy-start(s32[64,4]{0,1:T(4,128)} %param.16) | copy-start | bytes 3076
  16.6 17.7 %copy-start = (bf16[256,256]{1,0:T(8,128)(2,1)S(1)}, bf16[256,256]{1,0:T(8,128)(2,1)}, u32[]{:S(2)}) copy-start(bf16[256,256]{1,0:T(8,128)(2,1)} %constant.48.clone.pair) | copy-start | bytes 393220
  16.6 17.7 %copy-start.3 = (f32[4,16,128]{2,1,0:T(8,128)S(1)}, f32[4,16,128]{2,1,0:T(8,128)}, u32[]{:S(2)}) copy-start(f32[4,16,128]{2,1,0:T(8,128)} %constant.49.clone.picks) | copy-start | bytes 98308
  16.6 28.3 %collective-permute-start.3 = (f32[1,15,80,128]{3,2,1,0:T(8,128)}, f32[1,15,80,128]{3,2,1,0:T(8,128)}, u32[]{:S(2)}, u32[]{:S(2)}) collective-permute-start(f32[1,15,80,128]{3,2,1,0:T(8,128)} %get-tuple-element.33), channel_id=1, source_target_pairs={{1,2},{2,1},{5,6},{6,5},{9,10},{10,9},{13,14},{14,13},{17,18},{18,... | collective-permute-start | bytes 1843208 | tf_op jit(solution)/shard_map/ppermute | solution.py:510
  22.3 27.3 %collective-permute-start = (f32[1,15,80,128]{3,2,1,0:T(8,128)}, f32[1,15,80,128]{3,2,1,0:T(8,128)}, u32[]{:S(2)}, u32[]{:S(2)}) collective-permute-start(f32[1,15,80,128]{3,2,1,0:T(8,128)} %get-tuple-element.28), channel_id=1, source_target_pairs={{0,1},{1,0},{2,3},{3,2},{4,5},{5,4},{6,7},{7,6},{8,9},{9,8},{10,11... | collective-permute-start | bytes 1843208 | tf_op jit(solution)/shard_map/ppermute | solution.py:511
  22.3 36.9 %collective-permute-start.1 = (f32[1,15,80,128]{3,2,1,0:T(8,128)}, f32[1,15,80,128]{3,2,1,0:T(8,128)}, u32[]{:S(2)}, u32[]{:S(2)}) collective-permute-start(f32[1,15,80,128]{3,2,1,0:T(8,128)} %get-tuple-element.30), channel_id=1, source_target_pairs={{1,2},{2,1},{5,6},{6,5},{9,10},{10,9},{13,14},{14,13},{17,18},{18,... | collective-permute-start | bytes 1843208 | tf_op jit(solution)/shard_map/ppermute | solution.py:510
  38.8 6.1 %copy-start.2 = (f32[1,16,80,128]{3,2,1,0:T(8,128)S(1)}, f32[1,16,80,128]{3,2,1,0:T(8,128)}, u32[]{:S(2)}) copy-start(f32[1,16,80,128]{3,2,1,0:T(8,128)} %copy-done.1) | copy-start | bytes 1966084
  63.9 28.6 %copy-start.17 = (s32[64,4]{0,1:T(4,128)S(1)}, s32[64,4]{0,1:T(4,128)}, u32[]{:S(2)}) copy-start(s32[64,4]{0,1:T(4,128)} %param.17) | copy-start | bytes 3076
  63.9 29.1 %copy-start.16 = (s32[64,4]{0,1:T(4,128)S(1)}, s32[64,4]{0,1:T(4,128)}, u32[]{:S(2)}) copy-start(s32[64,4]{0,1:T(4,128)} %param.15) | copy-start | bytes 3076
  63.9 75.3 %copy-start.4 = (bf16[384,512]{1,0:T(8,128)(2,1)S(1)}, bf16[384,512]{1,0:T(8,128)(2,1)}, u32[]{:S(2)}) copy-start(bf16[384,512]{1,0:T(8,128)(2,1)} %constant.54.clone.corner) | copy-start | bytes 1179652
  63.9 75.3 %copy-start.5 = (bf16[32,128]{1,0:T(8,128)(2,1)S(1)}, bf16[32,128]{1,0:T(8,128)(2,1)}, u32[]{:S(2)}) copy-start(bf16[32,128]{1,0:T(8,128)(2,1)} %constant.55.clone.ends) | copy-start | bytes 24580
  63.9 75.3 %all-to-all-start = ((f32[64,4,16,128]{3,2,1,0:T(8,128)}), f32[64,4,16,128]{3,2,1,0:T(8,128)S(1)}, u32[]{:S(2)}, u32[]{:S(2)}) async-start(f32[64,4,16,128]{3,2,1,0:T(8,128)} %get-tuple-element.40), calls=%async_computation | async-start | bytes 4194304 | tf_op jit(solution)/shard_map/all_to_all | solution.py:528
  142.5 74.1 %all-to-all-start.1 = ((f32[64,4,16,128]{3,2,1,0:T(8,128)}), f32[64,4,16,128]{3,2,1,0:T(8,128)S(1)}, u32[]{:S(2)}, u32[]{:S(2)}) async-start(f32[64,4,16,128]{3,2,1,0:T(8,128)} %route.1), calls=%async_computation.1 | async-start | bytes 4194304 | tf_op jit(solution)/shard_map/all_to_all | solution.py:528
  150.6 14.1 %collective-permute-start.6 = (f32[2,15,48,128]{3,2,1,0:T(8,128)S(1)}, f32[2,15,48,128]{3,2,1,0:T(8,128)S(1)}, u32[]{:S(2)}, u32[]{:S(2)}) collective-permute-start(f32[2,15,48,128]{3,2,1,0:T(8,128)S(1)} %get-tuple-element.41), channel_id=1, source_target_pairs={{0,1},{1,0},{2,3},{3,2},{4,5},{5,4},{6,7},{7,6},{8,9},{9,8},{10,11... | collective-permute-start | bytes 2211848 | tf_op jit(solution)/shard_map/ppermute | solution.py:511
  150.7 46.3 %collective-permute-start.7 = (f32[2,15,48,128]{3,2,1,0:T(8,128)S(1)}, f32[2,15,48,128]{3,2,1,0:T(8,128)S(1)}, u32[]{:S(2)}, u32[]{:S(2)}) collective-permute-start(f32[2,15,48,128]{3,2,1,0:T(8,128)S(1)} %get-tuple-element.43), channel_id=1, source_target_pairs={{1,2},{2,1},{5,6},{6,5},{9,10},{10,9},{13,14},{14,13},{17,18},{18,... | collective-permute-start | bytes 2211848 | tf_op jit(solution)/shard_map/ppermute | solution.py:510
  162.3 36.4 %collective-permute-start.8 = (f32[2,15,48,128]{3,2,1,0:T(8,128)S(1)}, f32[2,15,48,128]{3,2,1,0:T(8,128)S(1)}, u32[]{:S(2)}, u32[]{:S(2)}) collective-permute-start(f32[2,15,48,128]{3,2,1,0:T(8,128)S(1)} %get-tuple-element.44), channel_id=1, source_target_pairs={{0,1},{1,0},{2,3},{3,2},{4,5},{5,4},{6,7},{7,6},{8,9},{9,8},{10,11... | collective-permute-start | bytes 2211848 | tf_op jit(solution)/shard_map/ppermute | solution.py:511
  162.4 42.5 %collective-permute-start.9 = (f32[2,15,48,128]{3,2,1,0:T(8,128)S(1)}, f32[2,15,48,128]{3,2,1,0:T(8,128)S(1)}, u32[]{:S(2)}, u32[]{:S(2)}) collective-permute-start(f32[2,15,48,128]{3,2,1,0:T(8,128)S(1)} %get-tuple-element.46), channel_id=1, source_target_pairs={{1,2},{2,1},{5,6},{6,5},{9,10},{10,9},{13,14},{14,13},{17,18},{18,... | collective-permute-start | bytes 2211848 | tf_op jit(solution)/shard_map/ppermute | solution.py:510
  198.7 7.9 %copy-start.11 = (f32[128,160]{1,0:T(8,128)S(1)}, f32[128,160]{1,0:T(8,128)}, u32[]{:S(2)}) copy-start(f32[128,160]{1,0:T(8,128)} %constant.50.clone.along) | copy-start | bytes 245764
  206.6 10.0 %copy-start.10 = (bf16[384,512]{1,0:T(8,128)(2,1)S(1)}, bf16[384,512]{1,0:T(8,128)(2,1)}, u32[]{:S(2)}) copy-start(bf16[384,512]{1,0:T(8,128)(2,1)} %constant.53.clone.spread) | copy-start | bytes 1179652
  206.6 10.0 %copy-start.12 = (bf16[2,128,128]{2,1,0:T(8,128)(2,1)S(1)}, bf16[2,128,128]{2,1,0:T(8,128)(2,1)}, u32[]{:S(2)}) copy-start(bf16[2,128,128]{2,1,0:T(8,128)(2,1)} %constant.51.clone.square) | copy-start | bytes 196612
  206.7 10.0 %copy-start.13 = (bf16[128,96]{1,0:T(8,128)(2,1)S(1)}, bf16[128,96]{1,0:T(8,128)(2,1)}, u32[]{:S(2)}) copy-start(bf16[128,96]{1,0:T(8,128)(2,1)} %constant.52.clone.ahead) | copy-start | bytes 73732
  (6 other events, 11.1 us)
